TPU v7x, 32 devices: a whole 2x2x4 slice. The times are simulated.
32 devices in a mesh: dp: 8 (over y, x, core), tensor: 4 (over z).
Axes of the slice: x: 2, y: 2, z: 4, core: 2. Of those that a mesh axis runs over, the one named last changes fastest.
Arguments:
- tokens: bfloat16 [16384, 768], P('dp'), may hold values from -6 to 6
- doc_lengths: int32 [16, 8], P('dp'), may hold values from 1 to 512, 1024 in all within a row
- wq: bfloat16 [768, 768], P('dp', 'tensor'), may hold values from -0.21875 to 0.21875
- bq: float32 [768], P('tensor'), may hold values from -3 to 3
- wk: bfloat16 [768, 768], P('dp', 'tensor'), may hold values from -0.21875 to 0.21875
- wv: bfloat16 [768, 768], P('dp', 'tensor'), may hold values from -0.21875 to 0.21875
- bv: float32 [768], P('tensor'), may hold values from -3 to 3
- wo: bfloat16 [768, 768], P('tensor', 'dp'), may hold values from -0.875 to 0.875
- bo: float32 [768], replicated, may hold values from -3 to 3
- gain1: float32 [768], replicated, may hold values from 0.25 to 1.75
- shift1: float32 [768], replicated, may hold values from -3 to 3
- w1: bfloat16 [768, 3072], P('dp', 'tensor'), may hold values from -0.21875 to 0.21875
- b1: float32 [3072], P('tensor'), may hold values from -3 to 3
- w2: bfloat16 [3072, 768], P('tensor', 'dp'), may hold values from -0.109375 to 0.109375
- b2: float32 [768], replicated, may hold values from -3 to 3
- gain2: float32 [768], replicated, may hold values from 0.25 to 1.75
- shift2: float32 [768], replicated, may hold values from -3 to 3
- cotangent: bfloat16 [16384, 768], P('dp'), may hold values from -6 to 6
Outputs:
- out: bfloat16 [16384, 768], P('dp')
- grad_tokens: bfloat16 [16384, 768], P('dp')
- grad_wq: float32 [768, 768], P('dp', 'tensor')
- grad_bq: float32 [768], P('tensor')
- grad_wk: float32 [768, 768], P('dp', 'tensor')
- grad_wv: float32 [768, 768], P('dp', 'tensor')
- grad_bv: float32 [768], P('tensor')
- grad_wo: float32 [768, 768], P('tensor', 'dp')
- grad_bo: float32 [768], replicated
- grad_gain1: float32 [768], replicated
- grad_shift1: float32 [768], replicated
- grad_w1: float32 [768, 3072], P('dp', 'tensor')
- grad_b1: float32 [3072], P('tensor')
- grad_w2: float32 [3072, 768], P('tensor', 'dp')
- grad_b2: float32 [768], replicated
- grad_gain2: float32 [768], replicated
- grad_shift2: float32 [768], replicated
Inputs may be any that keep to these rules, and one draw needn't show every extreme that they name: `doc_lengths`: row s holds the lengths of the documents packed in order into sequence s; each row sums to 1024.
All inputs are finite; a program needn't handle non-finite values.
Results may differ from a plain program's by a relative error of at most 0.02.
Values may be sent and summed in bfloat16 or wider, within the bound.
A program may use at most 192 MiB of HBM per device.

v0:
```python
from functools import partial

import jax
import jax.numpy as jnp
from jax import lax
from jax.sharding import PartitionSpec as P

HD = 64


eps_norm = 1e-12
masked_score = -1e30


def doc_ids(lengths, count):
    ends = jnp.cumsum(lengths)
    places = jnp.arange(count, dtype=jnp.int32)
    return jnp.sum((places[:, None] >= ends[None, :]).astype(jnp.int32), axis=1)


def collect(wq, wk, wv, wo, w1, w2):
    return (
        lax.all_gather(wq, "dp", axis=0, tiled=True),
        lax.all_gather(wk, "dp", axis=0, tiled=True),
        lax.all_gather(wv, "dp", axis=0, tiled=True),
        lax.all_gather(wo, "dp", axis=1, tiled=True),
        lax.all_gather(w1, "dp", axis=0, tiled=True),
        lax.all_gather(w2, "dp", axis=1, tiled=True),
    )


def reduce_large(grads):
    return (
        lax.psum_scatter(grads[0], "dp", scatter_dimension=0, tiled=True),
        lax.psum_scatter(grads[1], "dp", scatter_dimension=0, tiled=True),
        lax.psum_scatter(grads[2], "dp", scatter_dimension=0, tiled=True),
        lax.psum_scatter(grads[3], "dp", scatter_dimension=1, tiled=True),
        lax.psum_scatter(grads[4], "dp", scatter_dimension=0, tiled=True),
        lax.psum_scatter(grads[5], "dp", scatter_dimension=1, tiled=True),
    )


def reduce_small(grads):
    return lax.psum(
        (grads[0], grads[1], grads[2], grads[3], grads[4], grads[5], grads[6], grads[7], grads[8]),
        "dp",
    )


def contract_rows(left, right):
    return lax.dot_general(
        left, right, (((0,), (0,)), ((), ())), preferred_element_type=jnp.float32
    )


def contract_cols(left, right):
    return lax.dot_general(
        left, right, (((1,), (1,)), ((), ())), preferred_element_type=jnp.float32
    )


def contract_mixed(left, right):
    return lax.dot_general(
        left, right, (((0,), (1,)), ((), ())), preferred_element_type=jnp.float32
    )


def norm_forward(total, gain, shift):
    centre = total - jnp.mean(total, axis=-1, keepdims=True)
    scaled = lax.rsqrt(jnp.mean(centre * centre, axis=-1, keepdims=True) + eps_norm)
    normed = centre * scaled
    return (normed * gain + shift, normed, scaled)


def norm_backward(grad_result, normed, scaled, gain):
    grad_normed = grad_result * gain
    mean_grad = jnp.mean(grad_normed, axis=-1, keepdims=True)
    mean_cross = jnp.mean(grad_normed * normed, axis=-1, keepdims=True)
    grad_total = scaled * (grad_normed - mean_grad - normed * mean_cross)
    return (grad_total, jnp.sum(grad_result * normed, axis=0), jnp.sum(grad_result, axis=0))


def block_scores(query_block, key_heads, seg_block, seg, scale):
    raw = (
        jnp.einsum("hdq,hdk->hqk", query_block, key_heads, preferred_element_type=jnp.float32)
        * scale
    )
    same_doc = seg_block[:, None] == seg[None, :]
    return jnp.where(same_doc[None], raw, masked_score)


def body(
    tokens,
    doc_lengths,
    wq,
    bq,
    wk,
    wv,
    bv,
    wo,
    bo,
    gain1,
    shift1,
    w1,
    b1,
    w2,
    b2,
    gain2,
    shift2,
    cotangent,
):
    micro = doc_lengths.shape[0]
    seq_len = tokens.shape[0] // micro
    block = min(512, seq_len)
    scale = HD ** (-0.5)
    results = []
    grad_inputs = []
    large_total = None
    small_total = None
    for index in range(micro):
        full = collect(wq, wk, wv, wo, w1, w2)
        full_q, full_k, full_v, full_o, full_first, full_second = full
        width = full_q.shape[1]
        heads_here = width // HD
        rows_in = tokens[index * seq_len : (index + 1) * seq_len]
        inputs = rows_in.astype(jnp.float32)
        seg = doc_ids(doc_lengths[index], seq_len)
        queries = (
            lax.dot_general(
                full_q, rows_in, (((0,), (1,)), ((), ())), preferred_element_type=jnp.float32
            )
            + bq[:, None]
        ).astype(jnp.bfloat16)
        keys_low = lax.dot_general(
            full_k, rows_in, (((0,), (1,)), ((), ())), preferred_element_type=jnp.float32
        ).astype(jnp.bfloat16)
        values_low = (
            lax.dot_general(
                full_v, rows_in, (((0,), (1,)), ((), ())), preferred_element_type=jnp.float32
            )
            + bv[:, None]
        ).astype(jnp.bfloat16)
        query_heads = queries.reshape(heads_here, HD, seq_len)
        key_heads = keys_low.reshape(heads_here, HD, seq_len)
        value_heads = values_low.reshape(heads_here, HD, seq_len)
        pieces = []
        log_totals = []
        for offset in range(0, seq_len, block):
            scores = block_scores(
                query_heads[:, :, offset : offset + block],
                key_heads,
                seg[offset : offset + block],
                seg,
                scale,
            )
            highest = jnp.max(scores, axis=-1, keepdims=True)
            log_total = highest + jnp.log(
                jnp.sum(jnp.exp(scores - highest), axis=-1, keepdims=True)
            )
            probs_low = jnp.exp(scores - log_total).astype(jnp.bfloat16)
            pieces.append(
                jnp.einsum(
                    "hqk,hdk->hdq", probs_low, value_heads, preferred_element_type=jnp.float32
                )
            )
            log_totals.append(log_total)
        mixed_cols = jnp.concatenate(pieces, axis=2).reshape(width, seq_len).astype(jnp.bfloat16)
        attended = lax.psum(
            contract_rows(mixed_cols, full_o).astype(jnp.bfloat16), "tensor"
        ).astype(jnp.float32)
        first, normed_one, scaled_one = norm_forward(inputs + attended + bo, gain1, shift1)
        first_low = first.astype(jnp.bfloat16)
        inner = jnp.dot(first_low, full_first, preferred_element_type=jnp.float32) + b1
        hidden = jax.nn.gelu(inner, approximate=False).astype(jnp.bfloat16)
        second = lax.psum(
            jnp.dot(hidden, full_second, preferred_element_type=jnp.float32).astype(jnp.bfloat16),
            "tensor",
        ).astype(jnp.float32)
        result, normed_two, scaled_two = norm_forward(first + second + b2, gain2, shift2)
        results.append(result.astype(jnp.bfloat16))
        grad_result = cotangent[index * seq_len : (index + 1) * seq_len].astype(jnp.float32)
        grad_two, grad_gain2, grad_shift2 = norm_backward(
            grad_result, normed_two, scaled_two, gain2
        )
        grad_b2 = jnp.sum(grad_two, axis=0)
        full = collect(wq, wk, wv, wo, w1, w2)
        full_q, full_k, full_v, full_o, full_first, full_second = full
        two_low = grad_two.astype(jnp.bfloat16)
        grad_w2 = contract_rows(hidden, two_low)
        grad_hidden = contract_cols(two_low, full_second)
        grad_inner = jax.vjp(partial(jax.nn.gelu, approximate=False), inner)[1](grad_hidden)[
            0
        ].astype(jnp.bfloat16)
        grad_b1 = jnp.sum(grad_inner.astype(jnp.float32), axis=0)
        grad_w1 = contract_rows(first_low, grad_inner)
        grad_first = grad_two + lax.psum(
            contract_cols(grad_inner, full_first).astype(jnp.bfloat16), "tensor"
        ).astype(jnp.float32)
        grad_one, grad_gain1, grad_shift1 = norm_backward(grad_first, normed_one, scaled_one, gain1)
        grad_bo = jnp.sum(grad_one, axis=0)
        one_low = grad_one.astype(jnp.bfloat16)
        grad_wo = jnp.dot(mixed_cols, one_low, preferred_element_type=jnp.float32)
        grad_mixed = (
            contract_cols(full_o, one_low).astype(jnp.bfloat16).reshape(heads_here, HD, seq_len)
        )
        grad_key_heads = jnp.zeros((heads_here, HD, seq_len), jnp.float32)
        grad_value_heads = jnp.zeros((heads_here, HD, seq_len), jnp.float32)
        grad_query_pieces = []
        for number, offset in enumerate(range(0, seq_len, block)):
            query_block = query_heads[:, :, offset : offset + block]
            grad_block = grad_mixed[:, :, offset : offset + block]
            scores = block_scores(query_block, key_heads, seg[offset : offset + block], seg, scale)
            probs = jnp.exp(scores - log_totals[number])
            grad_probs = jnp.einsum(
                "hdq,hdk->hqk", grad_block, value_heads, preferred_element_type=jnp.float32
            )
            centre = jnp.sum(probs * grad_probs, axis=-1, keepdims=True)
            grad_scores = (probs * (grad_probs - centre)).astype(jnp.bfloat16)
            grad_query_pieces.append(
                jnp.einsum(
                    "hqk,hdk->hdq", grad_scores, key_heads, preferred_element_type=jnp.float32
                )
                * scale
            )
            grad_key_heads = (
                grad_key_heads
                + jnp.einsum(
                    "hqk,hdq->hdk", grad_scores, query_block, preferred_element_type=jnp.float32
                )
                * scale
            )
            grad_value_heads = grad_value_heads + jnp.einsum(
                "hqk,hdq->hdk",
                probs.astype(jnp.bfloat16),
                grad_block,
                preferred_element_type=jnp.float32,
            )
        grad_queries = (
            jnp.concatenate(grad_query_pieces, axis=2).reshape(width, seq_len).astype(jnp.bfloat16)
        )
        grad_keys = grad_key_heads.reshape(width, seq_len).astype(jnp.bfloat16)
        grad_values = grad_value_heads.reshape(width, seq_len).astype(jnp.bfloat16)
        grad_bq = jnp.sum(grad_queries.astype(jnp.float32), axis=1)
        grad_bv = jnp.sum(grad_values.astype(jnp.float32), axis=1)
        grad_wq = contract_cols(rows_in.T, grad_queries)
        grad_wk = contract_cols(rows_in.T, grad_keys)
        grad_wv = contract_cols(rows_in.T, grad_values)
        back_terms = (
            contract_mixed(grad_queries, full_q)
            + contract_mixed(grad_keys, full_k)
            + contract_mixed(grad_values, full_v)
        )
        grad_rows = grad_one + lax.psum(back_terms.astype(jnp.bfloat16), "tensor").astype(
            jnp.float32
        )
        grad_inputs.append(grad_rows.astype(jnp.bfloat16))
        large_local = (grad_wq, grad_wk, grad_wv, grad_wo, grad_w1, grad_w2)
        small_local = (
            grad_bq,
            grad_bv,
            grad_b1,
            grad_bo,
            grad_b2,
            grad_gain1,
            grad_shift1,
            grad_gain2,
            grad_shift2,
        )
        large_local = reduce_large(large_local)
        small_local = reduce_small(small_local)
        if large_total is None:
            large_total = large_local
            small_total = small_local
        else:
            large_total = jax.tree.map(jnp.add, large_total, large_local)
            small_total = jax.tree.map(jnp.add, small_total, small_local)
    grad_wq, grad_wk, grad_wv, grad_wo, grad_w1, grad_w2 = large_total
    (
        grad_bq,
        grad_bv,
        grad_b1,
        grad_bo,
        grad_b2,
        grad_gain1,
        grad_shift1,
        grad_gain2,
        grad_shift2,
    ) = small_total
    return (
        jnp.concatenate(results, axis=0),
        jnp.concatenate(grad_inputs, axis=0),
        grad_wq,
        grad_bq,
        grad_wk,
        grad_wv,
        grad_bv,
        grad_wo,
        grad_bo,
        grad_gain1,
        grad_shift1,
        grad_w1,
        grad_b1,
        grad_w2,
        grad_b2,
        grad_gain2,
        grad_shift2,
    )


def solution(mesh):
    placed = (
        P("dp", None),
        P("dp", None),
        P("dp", "tensor"),
        P("tensor"),
        P("dp", "tensor"),
        P("dp", "tensor"),
        P("tensor"),
        P("tensor", "dp"),
        P(),
        P(),
        P(),
        P("dp", "tensor"),
        P("tensor"),
        P("tensor", "dp"),
        P(),
        P(),
        P(),
        P("dp", None),
    )
    return jax.shard_map(
        body,
        mesh=mesh,
        in_specs=placed,
        out_specs=(
            P("dp", None),
            P("dp", None),
            P("dp", "tensor"),
            P("tensor"),
            P("dp", "tensor"),
            P("dp", "tensor"),
            P("tensor"),
            P("tensor", "dp"),
            P(),
            P(),
            P(),
            P("dp", "tensor"),
            P("tensor"),
            P("tensor", "dp"),
            P(),
            P(),
            P(),
        ),
        check_vma=False,
    )
```

profile of v0, /device:TPU:1, one launch (start us, length us, event | category | flops | bytes accessed | tf_op | source)
XLA Modules:
  0.0 841.7 jit_solution(16882995216697023067)
XLA Ops:
  8.1 11.4 %all_gather.12 = bf16[768,192]{1,0:T(8,128)(2,1)S(1)} all-gather(bf16[96,192]{1,0:T(8,128)(2,1)} %param.23), channel_id=1, replica_groups=mesh['dp'=8,'tensor'=4] {'dp'}, dimensions={0}, use_global_device_ids=true | all-gather | bytes 331776 | tf_op jit(solution)/shard_map/all_gather | solution.py:25
  24.0 9.4 %all_gather.14 = bf16[768,192]{1,0:T(8,128)(2,1)S(1)} all-gather(bf16[96,192]{1,0:T(8,128)(2,1)S(1)} %copy-done.92), channel_id=1, replica_groups=mesh['dp'=8,'tensor'=4] {'dp'}, dimensions={0}, use_global_device_ids=true | all-gather | bytes 331776 | tf_op jit(solution)/shard_map/all_gather | solution.py:24
  36.4 9.0 %all_gather.13 = bf16[768,192]{1,0:T(8,128)(2,1)S(1)} all-gather(bf16[96,192]{1,0:T(8,128)(2,1)S(1)} %copy-done.93), channel_id=1, replica_groups=mesh['dp'=8,'tensor'=4] {'dp'}, dimensions={0}, use_global_device_ids=true | all-gather | bytes 331776 | tf_op jit(solution)/shard_map/all_gather | solution.py:23
  50.1 9.3 %all_gather.15 = bf16[192,768]{0,1:T(8,128)(2,1)S(1)} all-gather(bf16[192,96]{0,1:T(8,128)(2,1)} %copy.42), channel_id=1, replica_groups=mesh['dp'=8,'tensor'=4] {'dp'}, dimensions={1}, use_global_device_ids=true | all-gather | bytes 331776 | tf_op jit(solution)/shard_map/all_gather | solution.py:26
  90.5 120.1 %all-reduce.16.cloned.1.call-done = (bf16[1024,768]{1,0:T(8,128)(2,1)}, bf16[1024,768]{1,0:T(8,128)(2,1)}) async-done(((bf16[1024,768]{1,0:T(8,128)(2,1)}, bf16[1024,768]{1,0:T(8,128)(2,1)}), (bf16[1024,768]{1,0:T(8,128)(2,1)}, bf16[1024,768]{1,0:T(8,128)(2,1)})) %all-reduce.16.cloned.1.call-update) | async-done | bytes 3145744 | tf_op jit(solution)/shard_map/psum | solution.py:168
  221.3 17.1 %multiply_convert_fusion.5 = (bf16[1024,768]{1,0:T(8,128)(2,1)}, f32[1024,768]{1,0:T(8,128)}, bf16[1024,768]{1,0:T(8,128)(2,1)}, f32[1024,768]{1,0:T(8,128)}, f32[1024,768]{1,0:T(8,128)}) fusion(f32[768]{0:T(1024)S(1)} %copy-done.119, f32[1024,768]{1,0:T(8,128)S(1)} %fusion.68, bf16[768,768]{1,0:T(8,128)(2,1)S(1)} %copy-done.115, f32[768]{0:T(1024)S(1)} %copy-done.110, ...), kind=kOutput, calls=%fused_computation.92 | convolution fusion | flops 1318846464 | bytes 20078592 | tf_op jit(solution)/shard_map/dot_general | solution.py:173
  238.5 4.5 convolution_convert_fusion.4
  245.6 120.6 %all-reduce.14.cloned.1.call-done = (bf16[1024,768]{1,0:T(8,128)(2,1)}, bf16[1024,768]{1,0:T(8,128)(2,1)}) async-done(((bf16[1024,768]{1,0:T(8,128)(2,1)}, bf16[1024,768]{1,0:T(8,128)(2,1)}), (bf16[1024,768]{1,0:T(8,128)(2,1)}, bf16[1024,768]{1,0:T(8,128)(2,1)})) %all-reduce.14.cloned.1.call-update) | async-done | bytes 3145744 | tf_op jit(solution)/shard_map/psum | solution.py:175
  366.1 5.2 fusion.131
  394.7 120.6 %all-reduce.12.cloned.1.call-done = (bf16[1024,768]{1,0:T(8,128)(2,1)}, bf16[1024,768]{1,0:T(8,128)(2,1)}) async-done(((bf16[1024,768]{1,0:T(8,128)(2,1)}, bf16[1024,768]{1,0:T(8,128)(2,1)}), (bf16[1024,768]{1,0:T(8,128)(2,1)}, bf16[1024,768]{1,0:T(8,128)(2,1)})) %all-reduce.12.cloned.1.call-update) | async-done | bytes 3145744 | tf_op jit(solution)/shard_map/psum | solution.py:196
  515.3 9.7 %multiply_reduce_fusion.5 = (f32[768]{0:T(1024)}, f32[1024]{0:T(1024)S(1)}, f32[1024]{0:T(1024)S(1)}, f32[768]{0:T(1024)}, f32[768]{0:T(1024)}, /*index=5*/f32[1...) fusion(f32[1024,768]{1,0:T(8,128)} %copy-done.18, bf16[1024,768]{1,0:T(8,128)(2,1)} %get-tuple-element.110, ...), kind=kLoop, calls=%fused_computation.57 | loop fusion | flops 24371456 | bytes 15782912 | tf_op jit(solution)/shard_map/reduce_sum | solution.py:80
  525.0 5.3 fusion.130
  537.0 4.4 multiply_reduce_fusion
  545.8 8.4 multiply_convert_fusion
  559.7 5.7 fusion.84
  565.5 4.4 multiply_reduce_fusion.2
  574.3 8.2 multiply_convert_fusion.2
  591.8 5.8 convert_reduce_fusion.4
  597.6 5.6 convert_reduce_fusion.5
  656.1 24.0 %all-reduce = (f32[192]{0:T(256)}, f32[192]{0:T(256)}, f32[768]{0:T(1024)}, f32[768]{0:T(1024)}, f32[768]{0:T(1024)}, /*index=5*/f32[768]{0:T(1024)}, f32[768]{0:T(1024)}, f32[768]{0:T(1024)}, f32[768]{0:T(1024)}) all-reduce(f32[192]{0:T(256)} %reshape.371, f32[192]{0:T(256)} %reshape.372, ...), channel_id=1, replica_groups=mesh['dp'=8,'tensor'=4] {'dp'}, use_global_device_ids=true, to_apply=%region_43.44 | all-reduce | flops 5760 | bytes 46080 | tf_op jit(solution)/shard_map/psum | solution.py:44
  681.7 54.7 %all-reduce.10.cloned.1.call-done = (bf16[1024,768]{1,0:T(8,128)(2,1)}, bf16[1024,768]{1,0:T(8,128)(2,1)}) async-done(((bf16[1024,768]{1,0:T(8,128)(2,1)}, bf16[1024,768]{1,0:T(8,128)(2,1)}), (bf16[1024,768]{1,0:T(8,128)(2,1)}, bf16[1024,768]{1,0:T(8,128)(2,1)})) %all-reduce.10.cloned.1.call-update) | async-done | bytes 3145744 | tf_op jit(solution)/shard_map/psum | solution.py:253
  742.5 14.4 %reduce-scatter.23.cloned.1.call-done = f32[96,192]{1,0:T(8,128)} async-done(((f32[768,192]{1,0:T(8,128)}), f32[96,192]{1,0:T(8,128)}) %reduce-scatter.23.cloned.1.call-update) | async-done | bytes 73744
  756.9 38.6 %reduce-scatter.19.cloned.1.call-done = f32[96,192]{1,0:T(8,128)} async-done(((f32[768,192]{1,0:T(8,128)}), f32[96,192]{1,0:T(8,128)}) %reduce-scatter.19.cloned.1.call-update) | async-done | bytes 73744
  795.5 38.6 %reduce-scatter.21.cloned.1.call-done = f32[96,192]{1,0:T(8,128)} async-done(((f32[768,192]{1,0:T(8,128)}), f32[96,192]{1,0:T(8,128)}) %reduce-scatter.21.cloned.1.call-update) | async-done | bytes 73744
  (435 shorter events, 169.5 us)
Async XLA Ops:
  8.0 14.5 %copy-start = (bf16[2048,768]{1,0:T(8,128)(2,1)S(1)}, bf16[2048,768]{1,0:T(8,128)(2,1)}, u32[]{:S(2)}) copy-start(bf16[2048,768]{1,0:T(8,128)(2,1)} %param.18) | copy-start | bytes 9437188
  8.0 14.5 %copy-start.121 = (f32[192]{0:T(256)S(1)}, f32[192]{0:T(256)}, u32[]{:S(2)}) copy-start(f32[192]{0:T(256)} %param.24) | copy-start | bytes 2308
  8.0 16.0 %copy-start.92 = (bf16[96,192]{1,0:T(8,128)(2,1)S(1)}, bf16[96,192]{1,0:T(8,128)(2,1)}, u32[]{:S(2)}) copy-start(bf16[96,192]{1,0:T(8,128)(2,1)} %param.22) | copy-start | bytes 110596
  8.1 202.5 %all-reduce.16.cloned.1.call-start = ((), (), s32[]{:S(2)}) async-start(), calls=%async_computation.17 | async-start | bytes 6291456 | tf_op jit(solution)/shard_map/psum | solution.py:168
  19.6 13.9 %copy-start.40 = (bf16[768,192]{1,0:T(8,128)(2,1)}, bf16[768,192]{1,0:T(8,128)(2,1)S(1)}, u32[]{:S(2)}) copy-start(bf16[768,192]{1,0:T(8,128)(2,1)S(1)} %all_gather.12) | copy-start | bytes 884740
  24.0 12.3 %copy-start.93 = (bf16[96,192]{1,0:T(8,128)(2,1)S(1)}, bf16[96,192]{1,0:T(8,128)(2,1)}, u32[]{:S(2)}) copy-start(bf16[96,192]{1,0:T(8,128)(2,1)} %param.20) | copy-start | bytes 110596
  24.0 21.3 %copy-start.122 = (f32[192]{0:T(256)S(1)}, f32[192]{0:T(256)}, u32[]{:S(2)}) copy-start(f32[192]{0:T(256)} %param.21) | copy-start | bytes 2308
  33.5 13.3 %copy-start.52 = (bf16[768,192]{1,0:T(8,128)(2,1)}, bf16[768,192]{1,0:T(8,128)(2,1)S(1)}, u32[]{:S(2)}) copy-start(bf16[768,192]{1,0:T(8,128)(2,1)S(1)} %all_gather.14) | copy-start | bytes 884740
  36.4 13.0 %copy-start.94 = (bf16[192,96]{1,0:T(8,128)(2,1)S(1)}, bf16[192,96]{1,0:T(8,128)(2,1)}, u32[]{:S(2)}) copy-start(bf16[192,96]{1,0:T(8,128)(2,1)} %param.25) | copy-start | bytes 110596
  86.6 124.0 %copy-start.78 = (f32[768]{0:T(1024)S(1)}, f32[768]{0:T(1024)}, u32[]{:S(2)}) copy-start(f32[768]{0:T(1024)} %param.26) | copy-start | bytes 9220
  89.2 126.5 %all-gather.3.cloned.1.call-start = ((), (), s32[]{:S(2)}) async-start(), calls=%async_computation.6 | async-start | bytes 1327104 | tf_op jit(solution)/shard_map/all_gather | solution.py:27
  89.8 148.6 %all-gather.5.cloned.1.call-start = ((), (), s32[]{:S(2)}) async-start(), calls=%async_computation.7 | async-start | bytes 1327104 | tf_op jit(solution)/shard_map/all_gather | solution.py:28
  90.4 275.7 %all-reduce.14.cloned.1.call-start = ((), (), s32[]{:S(2)}) async-start(), calls=%async_computation.16 | async-start | bytes 6291456 | tf_op jit(solution)/shard_map/psum | solution.py:175
  245.5 269.7 %all-reduce.12.cloned.1.call-start = ((), (), s32[]{:S(2)}) async-start(), calls=%async_computation.15 | async-start | bytes 6291456 | tf_op jit(solution)/shard_map/psum | solution.py:196
  394.6 285.5 %reduce-scatter.25.cloned.1.call-start = ((), (), s32[]{:S(2)}) async-start(), calls=%async_computation.13 | async-start | bytes 884736
  515.3 18.9 %slice-start.4 = ((s8[6291456]{0:T(1024)(128)(4,1)}), s8[4194304]{0:T(1024)(128)(4,1)S(1)}, s32[]{:S(2)}) async-start(s8[6291456]{0:T(1024)(128)(4,1)} %bitcast.113), calls=%async_computation.22 | async-start | bytes 8388608
  545.8 13.9 %copy-start.88 = (f32[3,512]{1,0:T(4,128)S(1)}, f32[3,512]{1,0:T(4,128)}, u32[]{:S(2)}) copy-start(f32[3,512]{1,0:T(4,128)} %copy-done.87) | copy-start | bytes 18436
  591.5 145.0 %all-reduce.10.cloned.1.call-start = ((), (), s32[]{:S(2)}) async-start(), calls=%async_computation.14 | async-start | bytes 6291456 | tf_op jit(solution)/shard_map/psum | solution.py:253
  597.6 14.5 %copy-start.57 = (bf16[3,64,1024]{2,1,0:T(8,128)(2,1)}, bf16[3,64,1024]{2,1,0:T(8,128)(2,1)S(1)}, u32[]{:S(2)}) copy-start(bf16[3,64,1024]{2,1,0:T(8,128)(2,1)S(1)} %get-tuple-element.176) | copy-start | bytes 1179652
  615.9 126.7 %reduce-scatter.17.cloned.1.call-start = ((), (), s32[]{:S(2)}) async-start(), calls=%async_computation.9 | async-start | bytes 2654208 | tf_op jit(solution)/shard_map/reduce_scatter | solution.py:39
  623.3 119.3 %reduce-scatter.15.cloned.1.call-start = ((), (), s32[]{:S(2)}) async-start(), calls=%async_computation.8 | async-start | bytes 2654208 | tf_op jit(solution)/shard_map/reduce_scatter | solution.py:38
  630.8 126.1 %reduce-scatter.23.cloned.1.call-start = ((), (), s32[]{:S(2)}) async-start(), calls=%async_computation.12 | async-start | bytes 884736
  636.1 159.4 %reduce-scatter.19.cloned.1.call-start = ((), (), s32[]{:S(2)}) async-start(), calls=%async_computation.10 | async-start | bytes 884736
  643.8 190.3 %reduce-scatter.21.cloned.1.call-start = ((), (), s32[]{:S(2)}) async-start(), calls=%async_computation.11 | async-start | bytes 884736
  (130 other events, 594.9 us)
Sparse Core Ops, SparseCore 0:
  89.4 121.1 all-reduce.15
  245.6 120.4 all-reduce.13
  394.7 120.4 all-reduce.11
  616.0 120.4 all-reduce.9
Sparse Core Ops, SparseCore 1:
  91.6 24.0 all-gather.2
  117.4 23.9 all-gather.4
  591.6 33.7 reduce-scatter.24
  629.3 42.5 reduce-scatter.16
  676.2 42.4 reduce-scatter.14
  722.4 34.5 reduce-scatter.22
  760.5 34.9 reduce-scatter.18
  799.1 34.9 reduce-scatter.20
where the time goes:
time: 850 us; the launch traced here: 842 us
  waiting for transfers between devices  509 us (60%)
  matrix products  153 us (18%)
  other arithmetic  75.5 us (9%)
  blocking collectives  63.1 us (7%)
  local copies, waits for them, and re-layouts  22.8 us (3%)
  between operations  17.4 us (2%)
    psum x1, waiting for transfers between devices, body(): lax.psum(jnp.dot(hidden, full_second, preferred_element_type=jnp.float32)...  121 us
    psum x1, waiting for transfers between devices, body(): lax.psum(contract_cols(grad_inner, full_first).astype(jnp.bfloat16), 'ten...  121 us
    psum x1, waiting for transfers between devices, body(): lax.psum(contract_rows(mixed_cols, full_o).astype(jnp.bfloat16), 'tensor')  120 us
    unnamed x16, waiting for transfers between devices  92.8 us
    psum x1, waiting for transfers between devices, body(): lax.psum(back_terms.astype(jnp.bfloat16), 'tensor').astype(jnp.float32)  54.7 us
    psum x1, blocking collectives, reduce_small(): lax.psum((grads[0], grads[1], grads[2], grads[3], grads[4], grads[5], gra...  24 us
    dot_general x12, matrix products, contract_cols(): lax.dot_general(left, right, (((1,), (1,)), ((), ())), preferred_element_...  21.3 us
    dot_general x2, matrix products, body(): jnp.dot(first_low, full_first, preferred_element_type=jnp.float32) + b1  21 us
  transfers between devices with their start and end apart: 12, of which 7 were waited for; matrix products, arithmetic and copies ran while one was open for 11% of the time, Pallas kernels for 0%

commit v1 on v0

--- a/solution.py
+++ b/solution.py
@@ -1,15 +1,718 @@
 from functools import partial
-
 import jax
 import jax.numpy as jnp
 from jax import lax
+from jax.experimental import pallas as pl
+from jax.experimental.pallas import tpu as pltpu
+
 from jax.sharding import PartitionSpec as P
 
+BF = jnp.bfloat16
+F32 = jnp.float32
+EPS = 1e-12
 HD = 64
-
-
-eps_norm = 1e-12
-masked_score = -1e30
+NEG = -1e30
+RB = 256
+
+
+def nn(a, b):
+    return jnp.dot(a, b, preferred_element_type=F32)
+
+
+def nt(a, b):
+    return lax.dot_general(a, b, (((1,), (1,)), ((), ())), preferred_element_type=F32)
+
+
+def rows(r, n=RB):
+    return pl.ds(pl.multiple_of(r * n, n), n)
+
+
+def mean_last(x):
+    return jnp.mean(x, axis=-1, keepdims=True)
+
+
+def colsum(x):
+    return jnp.sum(x, axis=0, keepdims=True)
+
+
+def fb_scratch(T, W, F, D, L):
+    M = L // 2
+    WP = 256
+    return [
+        pltpu.VMEM((T, M, WP), BF),
+        pltpu.VMEM((T, L, WP), BF),
+        pltpu.VMEM((T, L, WP), BF),
+        pltpu.VMEM((T, M, WP), BF),
+        pltpu.VMEM((T, M, WP), BF),
+        pltpu.VMEM((W, L), BF),
+        pltpu.VMEM((W, M), F32),
+        pltpu.VMEM((T * 4, 8, M), F32),
+        pltpu.VMEM((L, M), F32),
+        pltpu.VMEM((M, D), F32),
+        pltpu.VMEM((M, 128), F32),
+        pltpu.VMEM((M, D), BF),
+        pltpu.VMEM((T, M, F), BF),
+        pltpu.VMEM((T, M, F), BF),
+        pltpu.VMEM((M, D), F32),
+        pltpu.VMEM((M, D), F32),
+        pltpu.VMEM((M, D), BF),
+        pltpu.VMEM((D, M), BF),
+        pltpu.VMEM((D, L), BF),
+    ]
+
+
+def fb_kernel(half_axis, W_, X, COT, SG, BIAS, NP, OUT, GTO, GTP, G, SM,
+              q, k, v, mixed, dO, vT, oT, lse, bias, n1, r1, flow, hid, gp, sec, gz, low, lowT, xT):
+    T = W_.shape[1]
+    D = W_.shape[2]
+    L = X.shape[0]
+    M = L // 2
+    W = D // T
+    NH = W // HD
+    c = half_axis
+    own = c * M
+    oth = (1 - c) * M
+    scale = HD ** (-0.5)
+
+    def ownrows(r):
+        return pl.ds(pl.multiple_of(own + r * RB, RB), RB)
+
+    def othrows(r):
+        return pl.ds(pl.multiple_of(oth + r * RB, RB), RB)
+
+    SM[...] = jnp.zeros_like(SM)
+    key_doc = jnp.broadcast_to(SG[0:1, :], (128, L)).T
+    for i in range(M // 128):
+        query_doc = SG[0:1, pl.ds(pl.multiple_of(own + i * 128, 128), 128)]
+        bias[:, i * 128:(i + 1) * 128] = jnp.where(key_doc == query_doc, 0.0, NEG)
+
+    @pl.loop(0, T)
+    def _(t):
+        @pl.loop(0, L // RB)
+        def _(r):
+            xs = X[rows(r), :]
+            k[t, rows(r), 0:W] = nn(xs, W_[0, t, :, W:2 * W]).astype(BF)
+            v[t, rows(r), 0:W] = (nn(xs, W_[0, t, :, 2 * W:3 * W]) + BIAS[t, 2:3, 0:W]).astype(BF)
+
+        @pl.loop(0, M // RB)
+        def _(r):
+            xs = X[ownrows(r), :]
+            q[t, rows(r), 0:W] = (
+                (nn(xs, W_[0, t, :, 0:W]) + BIAS[t, 1:2, 0:W]).astype(BF) * BF(scale)
+            ).astype(BF)
+
+    lane = lax.broadcasted_iota(jnp.int32, (1, 128), 1)
+
+    def head(ref, t, rr, j):
+        if j % 2 == 0 and j == NH - 1:
+            return ref[t, rr, j * HD:(j + 1) * HD]
+        p = j // 2
+        return ref[t, rr, p * 128:(p + 1) * 128]
+
+    def only(block, j):
+        if block.shape[1] == HD:
+            return block
+        keep = (lane < HD) if j % 2 == 0 else (lane >= HD)
+        return jnp.where(keep, block, jnp.zeros_like(block))
+
+    everything = slice(None)
+    QC = RB
+
+    @pl.loop(0, T)
+    def _(t):
+        vT[...] = v[t, :, 0:W].T
+
+        @pl.loop(0, M // QC)
+        def _(i):
+            qs = rows(i, QC)
+            for j in range(NH):
+                s = nt(head(k, t, everything, j), only(head(q, t, qs, j), j)) + bias[:, qs]
+                m = jnp.max(s, axis=0, keepdims=True)
+                p = jnp.exp(s - m)
+                l = jnp.sum(p, axis=0, keepdims=True)
+                lse[t * 4 + j, :, qs] = jnp.broadcast_to(m + jnp.log(l), (8, QC))
+                o = nn(vT[j * HD:(j + 1) * HD, :], p.astype(BF))
+                oT[j * HD:(j + 1) * HD, qs] = o * (1.0 / l)
+
+        mixed[t, :, 0:W] = oT[...].T.astype(BF)
+
+    @pl.loop(0, M // RB)
+    def _(r):
+        z = X[ownrows(r), :].astype(F32) + NP[0:1, :]
+        for t in range(T):
+            z = z + nt(mixed[t, rows(r), 0:W], W_[0, t, :, 3 * W:4 * W])
+        cen = z - mean_last(z)
+        rs = lax.rsqrt(mean_last(cen * cen) + EPS)
+        n = cen * rs
+        n1[rows(r), :] = n
+        r1[rows(r), :] = jnp.broadcast_to(rs, (RB, 128))
+        flow[rows(r), :] = (n * NP[1:2, :] + NP[2:3, :]).astype(BF)
+
+    @pl.loop(0, T)
+    def _(t):
+        @pl.loop(0, M // RB)
+        def _(r):
+            rr = rows(r)
+            inner = nn(flow[rr, :], W_[1, t]) + BIAS[t, 0:1, :]
+            phi = 0.5 * (1.0 + lax.erf(inner * (2.0 ** -0.5)))
+            h = (inner * phi).astype(BF)
+            hid[t, rr, :] = h
+            gp[t, rr, :] = (phi + inner * (jnp.exp(-0.5 * inner * inner) * 0.3989422804014327)).astype(BF)
+            add = nt(h, W_[2, t])
+
+            @pl.when(t == 0)
+            def _():
+                sec[rr, :] = add
+
+            @pl.when(t > 0)
+            def _():
+                sec[rr, :] += add
+
+    @pl.loop(0, M // RB)
+    def _(r):
+        rr = rows(r)
+        z = n1[rr, :] * NP[1:2, :] + NP[2:3, :] + sec[rr, :] + NP[3:4, :]
+        cen = z - mean_last(z)
+        rs = lax.rsqrt(mean_last(cen * cen) + EPS)
+        n = cen * rs
+        OUT[rr, :] = (n * NP[4:5, :] + NP[5:6, :]).astype(BF)
+        ct = COT[rr, :].astype(F32)
+        g = ct * NP[4:5, :]
+        g2 = rs * (g - mean_last(g) - n * mean_last(g * n))
+        SM[16:17, :] += colsum(ct * n)
+        SM[17:18, :] += colsum(ct)
+        SM[13:14, :] += colsum(g2)
+        gz[rr, :] = g2
+        low[rr, :] = g2.astype(BF)
+
+    lowT[...] = low[...].T
+
+    @pl.loop(0, T)
+    def _(t):
+        @pl.loop(0, M // RB)
+        def _(r):
+            rr = rows(r)
+            gi = (nn(low[rr, :], W_[2, t]) * gp[t, rr, :].astype(F32)).astype(BF)
+            gp[t, rr, :] = gi
+            SM[pl.ds(8 + t, 1), :] += colsum(gi.astype(F32))
+            gz[rr, :] += nt(gi, W_[1, t])
+
+        @pl.loop(0, D // RB)
+        def _(r):
+            G[2, t, rows(r), :] = nn(lowT[rows(r), :], hid[t]).astype(BF)
+
+    lowT[...] = flow[...].T
+
+    @pl.loop(0, T)
+    def _(t):
+        @pl.loop(0, D // RB)
+        def _(r):
+            G[1, t, rows(r), :] = nn(lowT[rows(r), :], gp[t]).astype(BF)
+
+    @pl.loop(0, M // RB)
+    def _(r):
+        rr = rows(r)
+        gf = gz[rr, :]
+        n = n1[rr, :]
+        g = gf * NP[1:2, :]
+        g1 = r1[rr, 0:1] * (g - mean_last(g) - n * mean_last(g * n))
+        SM[14:15, :] += colsum(gf * n)
+        SM[15:16, :] += colsum(gf)
+        SM[12:13, :] += colsum(g1)
+        gz[rr, :] = g1
+        low[rr, :] = g1.astype(BF)
+
+    lowT[...] = low[...].T
+
+    @pl.loop(0, T)
+    def _(t):
+        @pl.loop(0, M // RB)
+        def _(r):
+            dO[t, rows(r), 0:W] = nn(low[rows(r), :], W_[0, t, :, 3 * W:4 * W]).astype(BF)
+
+        @pl.loop(0, D // RB)
+        def _(r):
+            G[0, t, rows(r), 3 * W:4 * W] = nn(lowT[rows(r), :], mixed[t, :, 0:W]).astype(BF)
+
+    @pl.loop(0, T)
+    def _(t):
+        vT[...] = k[t, :, 0:W].T
+        for pair in range((NH + 1) // 2):
+            heads = [j for j in (2 * pair, 2 * pair + 1) if j < NH]
+            wide = HD * len(heads)
+            dk = jnp.zeros((L, wide), F32)
+            dv = jnp.zeros((L, wide), F32)
+            for j in heads:
+                for i in range(M // QC):
+                    qs = slice(i * QC, (i + 1) * QC)
+                    qm = only(head(q, t, qs, j), j)
+                    om = only(head(dO, t, qs, j), j)
+                    s = nt(head(k, t, everything, j), qm) + bias[:, qs]
+                    p = jnp.exp(s - lse[t * 4 + j, 0:1, qs])
+                    dp = nt(head(v, t, everything, j), om)
+                    cen = jnp.sum(p * dp, axis=0, keepdims=True)
+                    ds = (p * (dp - cen)).astype(BF)
+                    dv = dv + nn(p.astype(BF), om)
+                    dk = dk + nn(ds, qm)
+                    oT[j * HD:(j + 1) * HD, qs] = nn(vT[j * HD:(j + 1) * HD, :], ds) * scale
+            lanes = slice(pair * 128, pair * 128 + wide)
+            k[t, :, lanes] = dk.astype(BF)
+            v[t, :, lanes] = dv.astype(BF)
+        dq = oT[...].T.astype(BF)
+        q[t, :, 0:W] = dq
+        SM[pl.ds(t, 1), 0:W] += colsum(dq.astype(F32))
+        SM[pl.ds(T + t, 1), 0:W] += colsum(v[t, :, 0:W].astype(F32))
+
+    xT[...] = X[...].T
+    lowT[...] = X[pl.ds(pl.multiple_of(own, RB), M), :].T
+
+    @pl.loop(0, T)
+    def _(t):
+        @pl.loop(0, D // RB)
+        def _(r):
+            rr = rows(r)
+            G[0, t, rr, 0:W] = nn(lowT[rr, :], q[t, :, 0:W]).astype(BF)
+            G[0, t, rr, W:2 * W] = nn(xT[rr, :], k[t, :, 0:W]).astype(BF)
+            G[0, t, rr, 2 * W:3 * W] = nn(xT[rr, :], v[t, :, 0:W]).astype(BF)
+
+    @pl.loop(0, M // RB)
+    def _(r):
+        acc = jnp.zeros((RB, D), F32)
+        for t in range(T):
+            acc = acc + nt(k[t, othrows(r), 0:W], W_[0, t, :, W:2 * W])
+            acc = acc + nt(v[t, othrows(r), 0:W], W_[0, t, :, 2 * W:3 * W])
+        GTP[rows(r), :] = acc.astype(BF)
+        acc = gz[rows(r), :]
+        for t in range(T):
+            acc = acc + nt(q[t, rows(r), 0:W], W_[0, t, :, 0:W])
+            acc = acc + nt(k[t, ownrows(r), 0:W], W_[0, t, :, W:2 * W])
+            acc = acc + nt(v[t, ownrows(r), 0:W], W_[0, t, :, 2 * W:3 * W])
+        GTO[rows(r), :] = acc
+
+
+MESH = pl.DeviceIdType.MESH
+
+
+def place():
+    dp = lax.axis_index("dp")
+    z = lax.axis_index("tensor")
+    core = dp % 2
+    xbit = (dp // 2) % 2
+    ybit = (dp // 4) % 2
+    return dp, z, core, dp + 1 - 2 * core, dp + 2 - 4 * xbit, dp + 4 - 8 * ybit
+
+
+def greet(devices):
+    barrier = pltpu.get_barrier_semaphore()
+    for device in devices:
+        pl.semaphore_signal(barrier, inc=1, device_id=device, device_id_type=MESH)
+    pl.semaphore_wait(barrier, len(devices))
+
+
+def remote(src, dst, send, recv, device):
+    return pltpu.make_async_remote_copy(
+        src_ref=src, dst_ref=dst, send_sem=send, recv_sem=recv, device_id=device, device_id_type=MESH
+    )
+
+
+def gather_kernel(PK, TOK, COT, SEG, BP, W_, X, CO, SG, BI,
+                  loc, zs, zr, os_, xr, yr, cr, fs, dr, ks, kr, bs, br, ts, tr):
+    dp, z, core, dpc, dpx, dpy = place()
+    T = W_.shape[1]
+    S = PK.shape[1]
+    SL = PK.shape[0]
+    L = X.shape[0]
+    M = L // 2
+    home = z // 2
+    greet([(dp, (z + d) % T) for d in range(1, T)] + [(dpx, z), (dpy, z), (dpc, z)])
+
+    def block(s, t, i):
+        return W_.at[s, t, pl.ds(pl.multiple_of(i * S, S), S), :]
+
+    def source(d):
+        return (z - d + T) % T
+
+    started = []
+
+    def go(copy):
+        copy.start()
+        started.append(copy)
+
+    def push_z(s):
+        for d in range(1, T):
+            go(remote(PK.at[s], block(s, z, dp), zs.at[s, d - 1], zr.at[s, d - 1], (dp, (z + d) % T)))
+
+    push_z(0)
+    seq = pl.ds(pl.multiple_of((z % 2) * L, L), L)
+    mine = pl.ds(pl.multiple_of((z % 2) * L + core * M, M), M)
+    other = pl.ds(pl.multiple_of((z % 2) * L + (1 - core) * M, M), M)
+    tok_out = remote(TOK.at[seq], X, ts.at[0], tr.at[0], (dpc, z))
+    cot_out = remote(COT.at[other], CO, ts.at[1], tr.at[1], (dpc, z))
+    seg_out = remote(SEG.at[z % 2], SG, ts.at[2], tr.at[2], (dpc, z))
+    tok_in = pltpu.make_async_copy(TOK.at[seq], X, loc.at[4])
+    cot_in = pltpu.make_async_copy(COT.at[mine], CO, loc.at[5])
+    seg_in = pltpu.make_async_copy(SEG.at[z % 2], SG, loc.at[6])
+
+    @pl.when(core == home)
+    def _():
+        for copy in (tok_out, cot_out, seg_out, tok_in, cot_in, seg_in):
+            copy.start()
+
+    local = [pltpu.make_async_copy(PK.at[s], block(s, z, dp), loc.at[s]) for s in range(SL)]
+    local.append(pltpu.make_async_copy(BP, BI.at[z], loc.at[3]))
+    for copy in local:
+        copy.start()
+    for d in range(1, T):
+        go(remote(BP, BI.at[z], bs.at[d - 1], br.at[d - 1], (dp, (z + d) % T)))
+
+    def send_own(s, d):
+        t = source(d)
+        src = PK.at[s] if d == 0 else block(s, t, dp)
+        go(remote(src, block(s, t, dp), os_.at[0, s, d], xr.at[s, d], (dpx, z)))
+        go(remote(src, block(s, t, dp), os_.at[1, s, d], yr.at[s, d], (dpy, z)))
+        go(remote(src, block(s, t, dp), os_.at[2, s, d], cr.at[0, s, d], (dpc, z)))
+
+    def pass_core(kind, s, d, i):
+        t = source(d)
+        go(remote(block(s, t, i), block(s, t, i), ks.at[kind - 1, s, d], cr.at[kind, s, d], (dpc, z)))
+
+    dpxy = dpx + dpy - dp
+
+    def wait_z(s, d):
+        remote(PK.at[s], block(s, source(d), dp), zs.at[s, d - 1], zr.at[s, d - 1], (dp, z)).wait_recv()
+
+    def take_x(s, d):
+        t = source(d)
+        remote(PK.at[s], block(s, t, dpx), os_.at[0, s, d], xr.at[s, d], (dpx, z)).wait_recv()
+        if d < T // 2:
+            go(remote(block(s, t, dpx), block(s, t, dpx), fs.at[s, d], dr.at[s, d], (dpy, z)))
+        pass_core(1, s, d, dpx)
+
+    def take_y(s, d):
+        t = source(d)
+        remote(PK.at[s], block(s, t, dpy), os_.at[1, s, d], yr.at[s, d], (dpy, z)).wait_recv()
+        if d >= T // 2:
+            go(remote(block(s, t, dpy), block(s, t, dpy), fs.at[s, d], dr.at[s, d], (dpx, z)))
+        pass_core(2, s, d, dpy)
+
+    def take_diag(s, d):
+        t = source(d)
+        remote(PK.at[s], block(s, t, dpxy), fs.at[s, d], dr.at[s, d], (dpx, z)).wait_recv()
+        pass_core(3, s, d, dpxy)
+
+    for s in range(SL):
+        send_own(s, 0)
+    pieces = [(s, d) for s in range(SL) for d in range(T)]
+    for step in range(len(pieces) + 3):
+        if step < len(pieces):
+            s, d = pieces[step]
+            if d:
+                wait_z(s, d)
+                send_own(s, d)
+            if d == T - 1 and s + 1 < SL:
+                push_z(s + 1)
+        if 1 <= step <= len(pieces):
+            s, d = pieces[step - 1]
+            take_x(s, d)
+            take_y(s, d)
+        if 3 <= step:
+            s, d = pieces[step - 3]
+            take_diag(s, d)
+    for s, d in pieces:
+        for kind, i in enumerate((dpc, dpx + dpc - dp, dpy + dpc - dp, dpxy + dpc - dp)):
+            remote(PK.at[s], block(s, source(d), i), ks.at[0, s, d], cr.at[kind, s, d], (dpc, z)).wait_recv()
+    for d in range(1, T):
+        remote(BP, BI.at[source(d)], bs.at[d - 1], br.at[d - 1], (dp, z)).wait_recv()
+    for copy in local:
+        copy.wait()
+
+    @pl.when(core == home)
+    def _():
+        for copy in (tok_in, cot_in, seg_in):
+            copy.wait()
+        for copy in (tok_out, cot_out, seg_out):
+            copy.wait_send()
+
+    @pl.when(core != home)
+    def _():
+        for copy in (tok_out, cot_out, seg_out):
+            copy.wait_recv()
+
+    for copy in started:
+        copy.wait_send()
+
+
+def gather_call(PK, TOK, COT, SEG, BP, T, L):
+    SL, S, D = PK.shape
+    any_ = pl.BlockSpec(memory_space=pl.ANY)
+    dma = pltpu.SemaphoreType.DMA
+    return pl.pallas_call(
+        gather_kernel,
+        in_specs=[any_] * 5,
+        out_specs=[any_] * 5,
+        out_shape=[
+            jax.ShapeDtypeStruct((SL, T, D, D), BF),
+            jax.ShapeDtypeStruct((L, D), BF),
+            jax.ShapeDtypeStruct((L // 2, D), BF),
+            jax.ShapeDtypeStruct(SEG.shape[1:], F32),
+            jax.ShapeDtypeStruct((T,) + BP.shape, F32),
+        ],
+        scratch_shapes=[
+            dma((7,)),
+            dma((SL, T - 1)), dma((SL, T - 1)),
+            dma((3, SL, T)), dma((SL, T)), dma((SL, T)), dma((4, SL, T)),
+            dma((SL, T)), dma((SL, T)),
+            dma((3, SL, T)), dma((1,)),
+            dma((T - 1,)), dma((T - 1,)),
+            dma((3,)), dma((3,)),
+        ],
+        compiler_params=pltpu.CompilerParams(collective_id=0, has_side_effects=True),
+    )(PK, TOK, COT, SEG, BP)
+
+
+def tail_kernel(G, OUT, GTO, GTP, SM, OF, GF, DQ, DK, DV, DO, D1, D2, BQ, BV, B1, VEC,
+                rgt, gtb, rc, r1, r2, rz, acc, ssend, srecv,
+                gs, gr, osem, orcv, osl, gsem, grcv, gsl, fwd, cs, cr, s1, q1, s2, q2, s3, q3, ms, mr):
+    dp, z, core, dpc, dpx, dpy = place()
+    dpxy = dpx + dpy - dp
+    T = G.shape[1]
+    SL = G.shape[0]
+    D = G.shape[2]
+    S = rz.shape[2]
+    M = OUT.shape[0]
+    W = D // T
+    flip = dpc - dp
+    greet([(dp, (z + d) % T) for d in range(1, T)] + [(dpc, (z + d) % T) for d in range(T)]
+          + [(dpx, z), (dpy, z)])
+    started = []
+
+    def go(copy):
+        copy.start()
+        started.append(copy)
+
+    part = remote(GTP, rgt, gs, gr, (dpc, z))
+    part.start()
+
+    home = z // 2
+    dest = dp - core + home
+
+    def where(zz, cc):
+        return pl.ds(pl.multiple_of(((zz % 2) * 2 + cc) * M, M), M)
+
+    def push(src, full, sems, recv, slots):
+        copies = []
+        for d in (1, 2):
+            for sign in (1, -1):
+                zz = z + sign * d
+                copies.append((zz, sign * d, remote(
+                    src, full.at[where(z, core)], sems.at[(d - 1) * 2 + (sign < 0)],
+                    recv.at[(z % 2) * 2 + core], (dest, (zz + T) % T))))
+        for d in (2, 1):
+            for zz, off, copy in copies:
+                if abs(off) == d:
+                    @pl.when((zz >= 0) & (zz < T))
+                    def _(copy=copy):
+                        copy.start()
+
+        @pl.when(core != home)
+        def _():
+            remote(src, full.at[where(z, core)], sems.at[4], recv.at[(z % 2) * 2 + core], (dpc, z)).start()
+
+        @pl.when(core == home)
+        def _():
+            pltpu.make_async_copy(src, full.at[where(z, core)], slots).start()
+
+        def finish():
+            for zz, off, copy in copies:
+                @pl.when((zz >= 0) & (zz < T))
+                def _(copy=copy):
+                    copy.wait_send()
+
+            @pl.when(core != home)
+            def _():
+                remote(src, full.at[where(z, core)], sems.at[4], recv.at[(z % 2) * 2 + core], (dpc, z)).wait_send()
+
+            @pl.when(core == home)
+            def _():
+                pltpu.make_async_copy(src, full.at[where(z, core)], slots).wait()
+
+        return finish
+
+    relay = ((core == 0) & (z == 2)) | ((core == 1) & (z == 1))
+    far = 3 * core
+    beyond = 3 - far
+
+    def got(src, full, recv, zz, cc):
+        remote(src, full.at[where(zz, cc)], gs, recv.at[(zz % 2) * 2 + cc], (dp, z)).wait_recv()
+
+    def hand_on(src, full, recv, base):
+        @pl.when(relay)
+        def _():
+            for cc in range(2):
+                got(src, full, recv, far, cc)
+                remote(full.at[where(far, cc)], full.at[where(far, cc)], fwd.at[base + cc],
+                       recv.at[(far % 2) * 2 + cc], (dp, beyond)).start()
+
+    def settle(src, full, recv, base):
+        for k in range(2):
+            for cc in range(2):
+                zz = core * 2 + k
+                @pl.when(jnp.logical_not((zz == z) & (core == cc)) & jnp.logical_not(relay & (zz == far)))
+                def _():
+                    got(src, full, recv, zz, cc)
+
+        @pl.when(relay)
+        def _():
+            for cc in range(2):
+                remote(full.at[where(far, cc)], full.at[where(far, cc)], fwd.at[base + cc],
+                       recv.at[(far % 2) * 2 + cc], (dp, beyond)).wait_send()
+
+    out_done = push(OUT, OF, osem, orcv, osl)
+
+    def rowsof(i):
+        return pl.ds(pl.multiple_of(i * S, S), S)
+
+    order = [2, 1, 0][:SL]
+    rel = (dp, dpx, dpy, dpxy)
+    for s in order:
+        for k in range(4):
+            go(remote(G.at[s, :, rowsof(rel[k] + flip), :], rc.at[s, k], cs.at[s, k], cr.at[s, k], (dpc, z)))
+
+    part.wait_recv()
+    gtb[...] = (GTO[...] + rgt[...].astype(F32)).astype(BF)
+    gt_done = push(gtb, GF, gsem, grcv, gsl)
+
+    acc[...] = SM[...]
+    friends = [(dpc, z), (dpx, z), (dpy, z), (dp, z + 1 - 2 * (z % 2)), (dp, (z + 2) % T)]
+
+    def small(step):
+        ssend[step] = acc[...]
+        go(remote(ssend.at[step], srecv.at[step], ms.at[step], mr.at[step], friends[step]))
+
+    def small_end(step):
+        remote(ssend.at[step], srecv.at[step], ms.at[step], mr.at[step], friends[step]).wait_recv()
+        acc[...] += srecv[step]
+
+    def add(dst, src):
+        @pl.loop(0, dst.shape[0])
+        def _(t):
+            dst[t] = (dst[t].astype(F32) + src[t].astype(F32)).astype(BF)
+
+    small(0)
+
+    def stage0(s):
+        for k in (3, 1, 2, 0):
+            remote(G.at[s, :, rowsof(dp), :], rc.at[s, k], cs.at[s, k], cr.at[s, k], (dpc, z)).wait_recv()
+            add(rc.at[s, k], G.at[s, :, rowsof(rel[k]), :])
+            if k == 3:
+                go(remote(rc.at[s, 3, 0:2], r1.at[s, 0], s1.at[s, 0], q1.at[s, 0], (dpy, z)))
+                go(remote(rc.at[s, 3, 2:4], r1.at[s, 1], s1.at[s, 1], q1.at[s, 1], (dpx, z)))
+            if k == 1:
+                go(remote(rc.at[s, 1, 2:4], r2.at[s, 0, 2:4], s2.at[s, 0], q2.at[s, 0], (dpx, z)))
+            if k == 2:
+                go(remote(rc.at[s, 2, 0:2], r2.at[s, 1, 0:2], s2.at[s, 1], q2.at[s, 1], (dpy, z)))
+
+    def stage1(s):
+        remote(rc.at[s, 3, 0:2], r1.at[s, 0], s1.at[s, 0], q1.at[s, 0], (dpy, z)).wait_recv()
+        add(rc.at[s, 1, 0:2], r1.at[s, 0])
+        go(remote(rc.at[s, 1, 0:2], r2.at[s, 0, 0:2], s2.at[s, 2], q2.at[s, 2], (dpx, z)))
+        remote(rc.at[s, 3, 2:4], r1.at[s, 1], s1.at[s, 1], q1.at[s, 1], (dpx, z)).wait_recv()
+        add(rc.at[s, 2, 2:4], r1.at[s, 1])
+        go(remote(rc.at[s, 2, 2:4], r2.at[s, 1, 2:4], s2.at[s, 3], q2.at[s, 3], (dpy, z)))
+
+    def stage2(s):
+        for k, part_ in ((0, slice(2, 4)), (1, slice(0, 2)), (2, slice(0, 2)), (3, slice(2, 4))):
+            remote(rc.at[s, 1, part_], r2.at[s, k % 2, part_], s2.at[s, k], q2.at[s, k], (dpx, z)).wait_recv()
+        add(rc.at[s, 0], r2.at[s, 0])
+        add(rc.at[s, 0], r2.at[s, 1])
+        for d in range(1, T):
+            zz = (z + d) % T
+            go(remote(rc.at[s, 0, zz], rz.at[s, d - 1], s3.at[s, d - 1], q3.at[s, d - 1], (dp, zz)))
+
+    def stage3(s):
+        total = rc[s, 0, z].astype(F32)
+        for d in range(1, T):
+            remote(rc.at[s, 0, 0], rz.at[s, d - 1], s3.at[s, d - 1], q3.at[s, d - 1], (dp, z)).wait_recv()
+            total = total + rz[s, d - 1].astype(F32)
+        if s == 0:
+            DQ[...] = total[:, 0:W]
+            DK[...] = total[:, W:2 * W]
+            DV[...] = total[:, 2 * W:3 * W]
+            DO[...] = total[:, 3 * W:4 * W].T
+        if s == 1:
+            D1[...] = total
+        if s == 2:
+            D2[...] = total.T
+
+    n = len(order)
+    for step in range(n + 3):
+        if step < n:
+            stage0(order[step])
+        if step < 5:
+            small_end(step)
+            if step < 4:
+                small(step + 1)
+        if 0 <= step - 1 < n:
+            stage1(order[step - 1])
+        if 0 <= step - 2 < n:
+            stage2(order[step - 2])
+        if step == 2:
+            hand_on(OUT, OF, orcv, 0)
+        if 0 <= step - 3 < n:
+            stage3(order[step - 3])
+    hand_on(gtb, GF, grcv, 2)
+    BQ[...] = acc[pl.ds(z, 1), 0:W]
+    BV[...] = acc[pl.ds(T + z, 1), 0:W]
+    B1[...] = acc[pl.ds(2 * T + z, 1), :]
+    VEC[...] = acc[3 * T:3 * T + 8, :]
+    settle(OUT, OF, orcv, 0)
+    settle(gtb, GF, grcv, 2)
+    out_done()
+    gt_done()
+    part.wait_send()
+    for copy in started:
+        copy.wait_send()
+
+
+def tail_call(G, OUT, GTO, GTP, SM, T, S, F):
+    SL, _, D, _ = G.shape
+    M = OUT.shape[0]
+    W = D // T
+    any_ = pl.BlockSpec(memory_space=pl.ANY)
+    vm = pl.BlockSpec(memory_space=pltpu.VMEM)
+    dma = pltpu.SemaphoreType.DMA
+    f32 = lambda *s: jax.ShapeDtypeStruct(s, F32)
+    return pl.pallas_call(
+        tail_kernel,
+        in_specs=[vm] * 5,
+        out_specs=[any_, any_] + [vm] * 10,
+        out_shape=[
+            jax.ShapeDtypeStruct((4 * M, D), BF),
+            jax.ShapeDtypeStruct((4 * M, D), BF),
+            f32(S, W), f32(S, W), f32(S, W), f32(W, S), f32(S, F), f32(F, S),
+            f32(1, W), f32(1, W), f32(1, F), f32(8, D),
+        ],
+        scratch_shapes=[
+            pltpu.VMEM((M, D), BF), pltpu.VMEM((M, D), BF),
+            pltpu.VMEM((SL, 4, T, S, D), BF),
+            pltpu.VMEM((SL, 2, 2, S, D), BF),
+            pltpu.VMEM((SL, 2, T, S, D), BF),
+            pltpu.VMEM((SL, T - 1, S, D), BF),
+            pltpu.VMEM(SM.shape, F32), pltpu.VMEM((5,) + SM.shape, F32), pltpu.VMEM((5,) + SM.shape, F32),
+            dma, dma,
+            dma((5,)), dma((4,)), dma,
+            dma((5,)), dma((4,)), dma,
+            dma((4,)),
+            dma((SL, 4)), dma((SL, 4)),
+            dma((SL, 2)), dma((SL, 2)),
+            dma((SL, 4)), dma((SL, 4)),
+            dma((SL, T - 1)), dma((SL, T - 1)),
+            dma((5,)), dma((5,)),
+        ],
+        compiler_params=pltpu.CompilerParams(
+            collective_id=1, has_side_effects=True, vmem_limit_bytes=60 << 20
+        ),
+    )(G, OUT, GTO, GTP, SM)
 
 
 def doc_ids(lengths, count):
@@ -67,7 +770,7 @@
 
 def norm_forward(total, gain, shift):
     centre = total - jnp.mean(total, axis=-1, keepdims=True)
-    scaled = lax.rsqrt(jnp.mean(centre * centre, axis=-1, keepdims=True) + eps_norm)
+    scaled = lax.rsqrt(jnp.mean(centre * centre, axis=-1, keepdims=True) + EPS)
     normed = centre * scaled
     return (normed * gain + shift, normed, scaled)
 
@@ -86,10 +789,10 @@
         * scale
     )
     same_doc = seg_block[:, None] == seg[None, :]
-    return jnp.where(same_doc[None], raw, masked_score)
-
-
-def body(
+    return jnp.where(same_doc[None], raw, NEG)
+
+
+def general_body(
     tokens,
     doc_lengths,
     wq,
@@ -307,6 +1010,53 @@
     )
 
 
+def compute_call(W_, X, CO, SG, BI, NP, T):
+    _, _, D, F = W_.shape
+    L = X.shape[0]
+    M = L // 2
+    vm = pl.BlockSpec(memory_space=pltpu.VMEM)
+
+    def kernel(*refs):
+        fb_kernel(lax.axis_index("dp") % 2, *refs)
+
+    return pl.pallas_call(
+        kernel,
+        in_specs=[vm] * 6,
+        out_specs=[vm] * 5,
+        out_shape=[
+            jax.ShapeDtypeStruct((M, D), BF),
+            jax.ShapeDtypeStruct((M, D), F32),
+            jax.ShapeDtypeStruct((M, D), BF),
+            jax.ShapeDtypeStruct(W_.shape, BF),
+            jax.ShapeDtypeStruct((24, D), F32),
+        ],
+        scratch_shapes=fb_scratch(T, D // T, F, D, L),
+        compiler_params=pltpu.CompilerParams(vmem_limit_bytes=63 << 20),
+    )(W_, X, CO, SG, BI, NP)
+
+
+def split_body(T, tokens, doc_lengths, wq, bq, wk, wv, bv, wo, bo, gain1, shift1, w1, b1, w2, b2,
+               gain2, shift2, cotangent):
+    micro = doc_lengths.shape[0]
+    L = tokens.shape[0] // micro
+    D = tokens.shape[1]
+    S, W = wq.shape
+    F = w1.shape[1]
+    packed = jnp.stack([jnp.concatenate([wq, wk, wv, wo.T], axis=1), w1, w2.T])
+    ends = jnp.cumsum(doc_lengths, axis=1)
+    spots = jnp.arange(L, dtype=jnp.int32)
+    seg = jnp.sum((spots[None, :, None] >= ends[:, None, :]).astype(F32), axis=2)
+    seg = jnp.broadcast_to(seg[:, None, :], (micro, 8, L))
+    row = lambda x: jnp.pad(x[None, :], ((0, 0), (0, D - x.shape[0])))
+    biases = jnp.concatenate([row(b1), row(bq), row(bv), jnp.zeros((5, D), F32)])
+    norms = jnp.stack([bo, gain1, shift1, b2, gain2, shift2, bo, bo])
+    W_, X, CO, SG, BI = gather_call(packed, tokens, cotangent, seg, biases, T, L)
+    out, gto, gtp, G, sm = compute_call(W_, X, CO, SG, BI, norms, T)
+    (full, grads, dq, dk, dv, do, d1, d2, gbq, gbv, gb1, vec) = tail_call(G, out, gto, gtp, sm, T, S, F)
+    return (full, grads, dq, gbq[0], dk, dv, gbv[0], do, vec[0], vec[2], vec[3], d1, gb1[0], d2,
+            vec[1], vec[4], vec[5])
+
+
 def solution(mesh):
     placed = (
         P("dp", None),
@@ -328,6 +1078,10 @@
         P(),
         P("dp", None),
     )
+    if mesh.shape["dp"] == 8 and mesh.shape["tensor"] == 4:
+        body = partial(split_body, mesh.shape["tensor"])
+    else:
+        body = general_body
     return jax.shard_map(
         body,
         mesh=mesh,

time: 850 us -> 404 us (0.48)
  waiting for transfers between devices: 509 us -> 0 us
  Pallas kernels: 0 us -> 375 us
  matrix products: 153 us -> 0 us
  other arithmetic: 75.5 us -> 6.36 us
  blocking collectives: 63.1 us -> 0 us
  between operations: 17.4 us -> 0.75 us
    psum x4 -> x0, waiting for transfers between devices: 416 us -> none  [the longest x1 121 us: body(): lax.psum(jnp.dot(hidden, full_second, preferred_element_type=jnp.float32)...]
    pallas_call x0 -> x3, Pallas kernels: none -> 375 us  [the longest x1 193 us: tail_call(): pl.pallas_call(tail_kernel, in_specs=[vm] * 5, out_specs=[any_, any_] + [...]
    dot_general x60 -> x0, matrix products: 153 us -> none  [the longest x12 21.3 us: contract_cols(): lax.dot_general(left, right, (((1,), (1,)), ((), ())), preferred_element_...]
    unnamed x16 -> x0, waiting for transfers between devices: 92.8 us -> none
    all_gather x4 -> x0, blocking collectives: 39.1 us -> none  [the longest x1 11.4 us: collect(): lax.all_gather(wv, 'dp', axis=0, tiled=True)]
    reduce_sum x17 -> x1, other arithmetic: 38 us -> 0.1 us  [split_body(): jnp.sum((spots[None, :, None] >= ends[:, None, :]).astype(F32), axis=2)]
    psum x1 -> x0, blocking collectives: 24 us -> none  [reduce_small(): lax.psum((grads[0], grads[1], grads[2], grads[3], grads[4], grads[5], gra...]
    convert_element_type x4 -> x0, other arithmetic: 19.8 us -> none  [the longest x2 16.6 us: body(): grad_scores = (probs * (grad_probs - centre)).astype(jnp.bfloat16)]
  transfers between devices with their start and end apart: 12 -> 0, of which waited for: 7 -> 0; matrix products, arithmetic and copies ran while one was open for 11% -> 0% of each run, Pallas kernels for 0% -> 0%
where the time goes in v1:
time: 404 us; the launch traced here: 403 us
  Pallas kernels  375 us (93%)
  local copies, waits for them, and re-layouts  20.6 us (5%)
  other arithmetic  6.36 us (2%)
    pallas_call x1, Pallas kernels, tail_call(): pl.pallas_call(tail_kernel, in_specs=[vm] * 5, out_specs=[any_, any_] + [...  193 us
    pallas_call x1, Pallas kernels, compute_call(): pl.pallas_call(kernel, in_specs=[vm] * 6, out_specs=[vm] * 5, out_shape=[...  108 us
    pallas_call x1, Pallas kernels, gather_call(): pl.pallas_call(gather_kernel, in_specs=[any_] * 5, out_specs=[any_] * 5,...  74.2 us
    unnamed x27, local copies, waits for them, and re-layouts  12.8 us

profile of v1, /device:TPU:1, one launch (start us, length us, event | category | flops | bytes accessed | tf_op | source)
XLA Modules:
  0.0 402.9 jit_solution(6007663341530283751)
XLA Ops:
  0.7 0.9 reduce_window_sum.11
  1.6 0.7 stack.39
  2.3 0.7 stack.40
  3.0 0.7 stack.41
  3.7 0.7 broadcast_in_dim.21
  4.4 0.7 stack.42
  5.0 0.7 stack.43
  5.7 0.7 stack.44
  6.4 0.6 stack.45.refs_5_
  7.2 1.4 fusion.BP
  8.5 0.9 copy.37
  10.1 0.9 maximum_bitcast_fusion
  11.0 1.8 pad_maximum_fusion.PK
  12.8 74.2 %shard_map.305 = (bf16[3,4,768,768]{3,2,1,0:T(8,128)(2,1)}, bf16[1024,768]{1,0:T(8,128)(2,1)}, bf16[512,768]{1,0:T(8,128)(2,1)}, f32[8,1024]{1,0:T(8,128)}, f32[4,8,768]{2,1,0:T(8,128)}) custom-call(bf16[3,96,768]{2,1,0:T(8,128)(2,1)} %pad_maximum_fusion.PK, bf16[2048,768]{1,0:T(8,128)(2,1)} %TOK.1, bf16[2048,768]{1,0:T(8,128)(2,1)} %COT.1, ...), custom_call_target="tpu_custom_call" | custom-call | tf_op jit(solution)/shard_map/pallas_call | solution.py:449
  87.0 108.3 %shard_map.306 = (bf16[512,768]{1,0:T(8,128)(2,1)}, f32[512,768]{1,0:T(8,128)}, bf16[512,768]{1,0:T(8,128)(2,1)}, bf16[3,4,768,768]{3,2,1,0:T(8,128)(2,1)}, f32[24,768]{1,0:T(8,128)}) custom-call(bf16[3,4,768,768]{3,2,1,0:T(8,128)(2,1)} %get-tuple-element.39.refs_0_, bf16[1024,768]{1,0:T(8,128)(2,1)} %get-tuple-element.40.refs_1_, ...), custom_call_target="tpu_custom_call" | custom-call | tf_op jit(solution)/shard_map/pallas_call | solution.py:1022
  195.3 192.8 %shard_map.307 = (bf16[2048,768]{1,0:T(8,128)(2,1)}, bf16[2048,768]{1,0:T(8,128)(2,1)}, f32[96,192]{1,0:T(8,128)}, f32[96,192]{1,0:T(8,128)}, f32[96,192]{1,0:T(...) custom-call(bf16[3,4,768,768]{3,2,1,0:T(8,128)(2,1)} %get-tuple-elem, ...), custom_call_target="tpu_custom_call" | custom-call | tf_op jit(solution)/shard_map/pallas_call | solution.py:685
  388.1 1.3 reduce.3
  389.4 1.6 slice_reduce_fusion
  391.0 1.9 copy.38
  392.9 3.9 copy.48
  396.8 1.7 copy.49
  398.5 0.6 copy.50
  399.7 0.6 copy.52
  402.2 0.7 copy.56
  (24 shorter events, 3.2 us)
Async XLA Ops:
  392.8 3.9 copy-start
  396.8 1.7 copy-start.5
  396.8 2.4 copy-start.7
  396.8 2.9 copy-start.4
  396.8 3.6 copy-start.3
  396.8 4.2 %copy-start.6 = (f32[1,192]{1,0:T(1,128)S(1)}, f32[1,192]{1,0:T(1,128)}, u32[]{:S(2)}) copy-start(f32[1,192]{1,0:T(1,128)} %get-tuple-element.55) | copy-start | bytes 2308
  396.8 4.8 %copy-start.2 = (f32[192,96]{1,0:T(8,128)S(1)}, f32[192,96]{1,0:T(8,128)}, u32[]{:S(2)}) copy-start(f32[192,96]{1,0:T(8,128)} %get-tuple-element.125) | copy-start | bytes 221188
  396.8 5.4 %copy-start.1 = (f32[96,768]{1,0:T(8,128)S(1)}, f32[96,768]{1,0:T(8,128)}, u32[]{:S(2)}) copy-start(f32[96,768]{1,0:T(8,128)} %get-tuple-element.129) | copy-start | bytes 884740

commit v2 on v0

--- a/solution.py
+++ b/solution.py
@@ -1,15 +1,763 @@
 from functools import partial
-
 import jax
 import jax.numpy as jnp
 from jax import lax
+from jax.experimental import pallas as pl
+from jax.experimental.pallas import tpu as pltpu
+
 from jax.sharding import PartitionSpec as P
 
+BF = jnp.bfloat16
+F32 = jnp.float32
+EPS = 1e-12
 HD = 64
-
-
-eps_norm = 1e-12
-masked_score = -1e30
+NEG = -1e30
+RB = 256
+
+
+def nn(a, b):
+    return jnp.dot(a, b, preferred_element_type=F32)
+
+
+def nt(a, b):
+    return lax.dot_general(a, b, (((1,), (1,)), ((), ())), preferred_element_type=F32)
+
+
+def rows(r, n=RB):
+    return pl.ds(pl.multiple_of(r * n, n), n)
+
+
+def mean_last(x):
+    return jnp.mean(x, axis=-1, keepdims=True)
+
+
+def colsum(x):
+    return jnp.sum(x, axis=0, keepdims=True)
+
+
+MESH = pl.DeviceIdType.MESH
+
+
+def remote(src, dst, send, recv, device):
+    return pltpu.make_async_remote_copy(
+        src_ref=src, dst_ref=dst, send_sem=send, recv_sem=recv, device_id=device, device_id_type=MESH
+    )
+
+
+def layer_kernel(
+    WQ, WK, WV, WO, W1, W2T, NP, BP, LEN, TOK, COT,
+    OF, GF, DQ, DK, DV, DO, D1, D2, BQ, BV, B1, VEC,
+    PK, W_, G0, X, CO, SG, BI, SM,
+    q, k, v, mixed, vT, oT, lse, bias, n1, r1, flow, hid, gp, gz, low, xT, outb,
+    rgt, rc, ra, rb, rz, ssend, srecv,
+    loc, zs, zr, os_, xr, yr, cr, fs, dr, ks, bs, br, ts, tr,
+    gs, gr, osem, orcv, osl, gsem, grcv, gsl, fwd, cs, crr, s1, q1, s2, q2, s3, q3, ms, mr,
+):
+    SL, S, D = PK.shape
+    T = W_.shape[1]
+    L = X.shape[0]
+    M = L // 2
+    W = D // T
+    NH = W // HD
+    scale = HD ** (-0.5)
+    QC = RB
+
+    dp = lax.axis_index("dp")
+    z = lax.axis_index("tensor")
+    core = dp % 2
+    dpc = dp + 1 - 2 * core
+    dpx = dp + 2 - 4 * ((dp // 2) % 2)
+    dpy = dp + 4 - 8 * ((dp // 4) % 2)
+    dpxy = dpx + dpy - dp
+    flip = dpc - dp
+    home = z // 2
+    own = core * M
+    oth = (1 - core) * M
+
+    def ownrows(r):
+        return pl.ds(pl.multiple_of(own + r * RB, RB), RB)
+
+    def othrows(r):
+        return pl.ds(pl.multiple_of(oth + r * RB, RB), RB)
+
+    PK[0, :, 0:W] = WQ[...]
+    PK[0, :, W:2 * W] = WK[...]
+    PK[0, :, 2 * W:3 * W] = WV[...]
+    PK[0, :, 3 * W:4 * W] = WO[...].T
+    PK[1] = W1[...]
+    PK[2] = W2T[...]
+
+    spot = lax.broadcasted_iota(jnp.int32, (8, L), 1)
+    doc = jnp.zeros((8, L), F32)
+    end = jnp.int32(0)
+    for j in range(LEN.shape[1]):
+        end = end + LEN[z % 2, j]
+        doc = doc + jnp.where(spot >= end, 1.0, 0.0)
+    SG[0] = doc
+
+    barrier = pltpu.get_barrier_semaphore()
+    friends = [(dp, (z + d) % T) for d in range(1, T)] + [(dpc, (z + d) % T) for d in range(T)] + [
+        (dpx, z), (dpy, z)]
+    for friend in friends:
+        pl.semaphore_signal(barrier, inc=1, device_id=friend, device_id_type=MESH)
+    pl.semaphore_wait(barrier, len(friends))
+
+    def block(s, t, i):
+        return W_.at[s, t, pl.ds(pl.multiple_of(i * S, S), S), :]
+
+    def source(d):
+        return (z - d + T) % T
+
+    def push_z(s):
+        for d in range(1, T):
+            remote(PK.at[s], block(s, z, dp), zs.at[s, d - 1], zr.at[s, d - 1], (dp, (z + d) % T)).start()
+
+    def send_block(s, d, src):
+        t = source(d)
+        remote(src, block(s, t, dp), os_.at[0, s, d], xr.at[s, d], (dpx, z)).start()
+        remote(src, block(s, t, dp), os_.at[1, s, d], yr.at[s, d], (dpy, z)).start()
+        remote(src, block(s, t, dp), os_.at[2, s, d], cr.at[0, s, d], (dpc, z)).start()
+
+    def pass_core(kind, s, d, i):
+        t = source(d)
+        remote(block(s, t, i), block(s, t, i), ks.at[kind - 1, s, d], cr.at[kind, s, d], (dpc, z)).start()
+
+    def wait_z(s, d):
+        remote(PK.at[s], block(s, source(d), dp), zs.at[s, d - 1], zr.at[s, d - 1], (dp, (z + 1) % T)).wait_recv()
+
+    def take_x(s, d):
+        t = source(d)
+        remote(PK.at[s], block(s, t, dpx), os_.at[0, s, d], xr.at[s, d], (dpx, z)).wait_recv()
+
+        @pl.when(d < T // 2)
+        def _():
+            remote(block(s, t, dpx), block(s, t, dpx), fs.at[s, d], dr.at[s, d], (dpy, z)).start()
+
+        pass_core(1, s, d, dpx)
+
+    def take_y(s, d):
+        t = source(d)
+        remote(PK.at[s], block(s, t, dpy), os_.at[1, s, d], yr.at[s, d], (dpy, z)).wait_recv()
+
+        @pl.when(d >= T // 2)
+        def _():
+            remote(block(s, t, dpy), block(s, t, dpy), fs.at[s, d], dr.at[s, d], (dpx, z)).start()
+
+        pass_core(2, s, d, dpy)
+
+    def take_diag(s, d):
+        remote(PK.at[s], block(s, source(d), dpxy), fs.at[s, d], dr.at[s, d], (dpx, z)).wait_recv()
+        pass_core(3, s, d, dpxy)
+
+    PIECES = SL * T
+
+    def gather_step(n):
+        n = jnp.int32(n)
+
+        @pl.when(n < PIECES)
+        def _():
+            s, d = n // T, n % T
+
+            @pl.when(d > 0)
+            def _():
+                wait_z(s, d)
+                send_block(s, d, block(s, source(d), dp))
+
+            @pl.when((d == T - 1) & (s + 1 < SL))
+            def _():
+                push_z(s + 1)
+
+        @pl.when((n >= 1) & (n <= PIECES))
+        def _():
+            take_x((n - 1) // T, (n - 1) % T)
+            take_y((n - 1) // T, (n - 1) % T)
+
+        @pl.when((n >= 3) & (n < PIECES + 3))
+        def _():
+            take_diag((n - 3) // T, (n - 3) % T)
+
+    def gathered(s):
+        for d in range(T):
+            for kind, i in enumerate((dpc, dpx + flip, dpy + flip, dpxy + flip)):
+                remote(PK.at[s], block(s, source(d), i), os_.at[2, s, d], cr.at[kind, s, d], (dpc, z)).wait_recv()
+
+    push_z(0)
+    seq = pl.ds(pl.multiple_of((z % 2) * L, L), L)
+    mine = pl.ds(pl.multiple_of((z % 2) * L + own, M), M)
+    other = pl.ds(pl.multiple_of((z % 2) * L + oth, M), M)
+    tok_out = remote(TOK.at[seq], X, ts.at[0], tr.at[0], (dpc, z))
+    cot_out = remote(COT.at[other], CO, ts.at[1], tr.at[1], (dpc, z))
+    doc_out = remote(SG.at[0], SG.at[1], ts.at[2], tr.at[2], (dpc, z))
+    tok_in = pltpu.make_async_copy(TOK.at[seq], X, loc.at[0])
+    cot_in = pltpu.make_async_copy(COT.at[mine], CO, loc.at[1])
+
+    @pl.when(core == home)
+    def _():
+        for copy in (tok_out, cot_out, doc_out, tok_in, cot_in):
+            copy.start()
+
+    for d in range(1, T):
+        remote(BP, BI.at[z], bs.at[d - 1], br.at[d - 1], (dp, (z + d) % T)).start()
+    for s in range(SL):
+        send_block(s, 0, PK.at[s])
+        W_[s, z, pl.ds(pl.multiple_of(dp * S, S), S), :] = PK[s]
+    BI[z] = BP[...]
+    SM[...] = jnp.zeros_like(SM)
+
+    @pl.loop(0, T + 1)
+    def _(n):
+        gather_step(n)
+
+    @pl.when(core == home)
+    def _():
+        tok_in.wait()
+        cot_in.wait()
+        for copy in (tok_out, cot_out, doc_out):
+            copy.wait_send()
+
+    @pl.when(core != home)
+    def _():
+        for copy in (tok_out, cot_out, doc_out):
+            copy.wait_recv()
+
+    for d in range(1, T):
+        remote(BP, BI.at[source(d)], bs.at[d - 1], br.at[d - 1], (dp, (z + 1) % T)).wait_recv()
+
+    docs = jnp.where(core == home, SG[0], SG[1])
+    SG[0] = docs
+    key_doc = jnp.broadcast_to(docs[0:1, :], (128, L)).T
+    for i in range(M // 128):
+        query_doc = SG[0, 0:1, pl.ds(pl.multiple_of(own + i * 128, 128), 128)]
+        bias[:, i * 128:(i + 1) * 128] = jnp.where(key_doc == query_doc, 0.0, NEG)
+
+    @pl.loop(T + 1, T + 3)
+    def _(n):
+        gather_step(n)
+
+    gathered(0)
+
+    @pl.loop(0, T)
+    def _(t):
+        @pl.loop(0, L // RB)
+        def _(r):
+            xs = X[rows(r), :]
+            k[t, rows(r), 0:W] = nn(xs, W_[0, t, :, W:2 * W]).astype(BF)
+            v[t, rows(r), 0:W] = (nn(xs, W_[0, t, :, 2 * W:3 * W]) + BI[t, 2:3, 0:W]).astype(BF)
+
+        @pl.loop(0, M // RB)
+        def _(r):
+            xs = X[ownrows(r), :]
+            q[t, rows(r), 0:W] = (
+                (nn(xs, W_[0, t, :, 0:W]) + BI[t, 1:2, 0:W]).astype(BF) * BF(scale)
+            ).astype(BF)
+
+    lane = lax.broadcasted_iota(jnp.int32, (1, 128), 1)
+
+    def head(ref, t, rr, j):
+        if j % 2 == 0 and j == NH - 1:
+            return ref[t, rr, j * HD:(j + 1) * HD]
+        p = j // 2
+        return ref[t, rr, p * 128:(p + 1) * 128]
+
+    def only(part, j):
+        if part.shape[1] == HD:
+            return part
+        keep = (lane < HD) if j % 2 == 0 else (lane >= HD)
+        return jnp.where(keep, part, jnp.zeros_like(part))
+
+    everything = slice(None)
+
+    @pl.loop(0, T)
+    def _(t):
+        gather_step(T + 3 + t)
+        vT[...] = v[t, :, 0:W].T
+
+        @pl.loop(0, M // QC)
+        def _(i):
+            qs = rows(i, QC)
+            for j in range(NH):
+                s = nt(head(k, t, everything, j), only(head(q, t, qs, j), j)) + bias[:, qs]
+                m = jnp.max(s, axis=0, keepdims=True)
+                p = jnp.exp(s - m)
+                l = jnp.sum(p, axis=0, keepdims=True)
+                lse[t * 4 + j, :, qs] = jnp.broadcast_to(m + jnp.log(l), (8, QC))
+                o = nn(vT[j * HD:(j + 1) * HD, :], p.astype(BF))
+                oT[j * HD:(j + 1) * HD, qs] = o * (1.0 / l)
+
+        mixed[t, :, 0:W] = oT[...].T.astype(BF)
+
+    @pl.loop(0, M // RB)
+    def _(r):
+        zz = X[ownrows(r), :].astype(F32) + NP[0:1, :]
+        for t in range(T):
+            zz = zz + nt(mixed[t, rows(r), 0:W], W_[0, t, :, 3 * W:4 * W])
+        cen = zz - mean_last(zz)
+        rs = lax.rsqrt(mean_last(cen * cen) + EPS)
+        n = cen * rs
+        n1[rows(r), :] = n
+        r1[rows(r), :] = jnp.broadcast_to(rs, (RB, 128))
+        flow[rows(r), :] = (n * NP[1:2, :] + NP[2:3, :]).astype(BF)
+
+    gather_step(2 * T + 3)
+    gathered(1)
+
+    @pl.loop(0, T)
+    def _(t):
+        @pl.when(t < T - 1)
+        def _():
+            gather_step(2 * T + 4 + t)
+
+        @pl.loop(0, M // RB)
+        def _(r):
+            rr = rows(r)
+            inner = nn(flow[rr, :], W_[1, t]) + BI[t, 0:1, :]
+            phi = 0.5 * (1.0 + lax.erf(inner * (2.0 ** -0.5)))
+            hid[t, rr, :] = (inner * phi).astype(BF)
+            gp[t, rr, :] = (phi + inner * (jnp.exp(-0.5 * inner * inner) * 0.3989422804014327)).astype(BF)
+
+    gathered(2)
+
+    @pl.loop(0, M // RB)
+    def _(r):
+        rr = rows(r)
+        zz = n1[rr, :] * NP[1:2, :] + NP[2:3, :] + NP[3:4, :]
+        for t in range(T):
+            zz = zz + nt(hid[t, rr, :], W_[2, t])
+        cen = zz - mean_last(zz)
+        rs = lax.rsqrt(mean_last(cen * cen) + EPS)
+        n = cen * rs
+        outb[rr, :] = (n * NP[4:5, :] + NP[5:6, :]).astype(BF)
+        ct = CO[rr, :].astype(F32)
+        g = ct * NP[4:5, :]
+        g2 = rs * (g - mean_last(g) - n * mean_last(g * n))
+        SM[16:17, :] += colsum(ct * n)
+        SM[17:18, :] += colsum(ct)
+        SM[13:14, :] += colsum(g2)
+        gz[rr, :] = g2
+        low[rr, :] = g2.astype(BF)
+
+    dest = dp - core + home
+
+    def spotrows(zz, cc):
+        return pl.ds(pl.multiple_of(((zz % 2) * 2 + cc) * M, M), M)
+
+    def pushes(src, full, sems, recv):
+        copies = []
+        for d in (2, 1):
+            for sign in (1, -1):
+                zz = z + sign * d
+                copies.append((zz, remote(
+                    src, full.at[spotrows(z, core)], sems.at[(d - 1) * 2 + (sign < 0)],
+                    recv.at[(z % 2) * 2 + core], (dest, (zz + T) % T))))
+        return copies
+
+    def own_copy(src, full, sems, recv, slot):
+        away = remote(src, full.at[spotrows(z, core)], sems.at[4], recv.at[(z % 2) * 2 + core], (dpc, z))
+        here = pltpu.make_async_copy(src, full.at[spotrows(z, core)], slot)
+        return away, here
+
+    def push(src, full, sems, recv, slot):
+        for zz, copy in pushes(src, full, sems, recv):
+            pl.when((zz >= 0) & (zz < T))(copy.start)
+        away, here = own_copy(src, full, sems, recv, slot)
+        pl.when(core != home)(away.start)
+        pl.when(core == home)(here.start)
+
+    def pushed(src, full, sems, recv, slot):
+        for zz, copy in pushes(src, full, sems, recv):
+            pl.when((zz >= 0) & (zz < T))(copy.wait_send)
+        away, here = own_copy(src, full, sems, recv, slot)
+        pl.when(core != home)(away.wait_send)
+        pl.when(core == home)(here.wait)
+
+    relay = ((core == 0) & (z == 2)) | ((core == 1) & (z == 1))
+    far = 3 * core
+    beyond = 3 - far
+
+    def got(src, full, recv, zz, cc):
+        remote(src, full.at[spotrows(zz, cc)], gs, recv.at[(zz % 2) * 2 + cc], (dpx, z)).wait_recv()
+
+    def handing(full, recv, base, cc):
+        return remote(full.at[spotrows(far, cc)], full.at[spotrows(far, cc)], fwd.at[base + cc],
+                      recv.at[(far % 2) * 2 + cc], (dp, beyond))
+
+    def hand_on(src, full, recv, base):
+        @pl.when(relay)
+        def _():
+            for cc in range(2):
+                got(src, full, recv, far, cc)
+                handing(full, recv, base, cc).start()
+
+    def settle(src, full, recv, base):
+        for kk in range(2):
+            for cc in range(2):
+                zz = core * 2 + kk
+
+                @pl.when(jnp.logical_not((zz == z) & (core == cc)) & jnp.logical_not(relay & (zz == far)))
+                def _():
+                    got(src, full, recv, zz, cc)
+
+        @pl.when(relay)
+        def _():
+            for cc in range(2):
+                handing(full, recv, base, cc).wait_send()
+
+    push(outb, OF, osem, orcv, osl)
+
+    for s in range(SL):
+        for d in range(1, T):
+            remote(PK.at[s], block(s, z, dp), zs.at[s, d - 1], zr.at[s, d - 1], (dp, (z + d) % T)).wait_send()
+        for d in range(T):
+            for kind in range(3):
+                remote(PK.at[s], block(s, z, dp), os_.at[kind, s, d], xr.at[s, d], (dpx, z)).wait_send()
+                remote(PK.at[s], block(s, z, dp), ks.at[kind, s, d], xr.at[s, d], (dpx, z)).wait_send()
+            remote(PK.at[s], block(s, z, dp), fs.at[s, d], xr.at[s, d], (dpx, z)).wait_send()
+    for d in range(1, T):
+        remote(BP, BI.at[z], bs.at[d - 1], br.at[d - 1], (dp, (z + d) % T)).wait_send()
+
+    def grad(s):
+        return G0 if s == 0 else W_.at[s]
+
+    rel = (dp, dpx, dpy, dpxy)
+
+    def rowsof(i):
+        return pl.ds(pl.multiple_of(i * S, S), S)
+
+    def core_copy(s, kk):
+        return remote(grad(s).at[:, rowsof(rel[kk] + flip), :], rc.at[s, kk], cs.at[s, kk], crr.at[s, kk], (dpc, z))
+
+    def turn(s, kk):
+        src, dst, who = (
+            (rc.at[s, 3, 0:2], ra.at[s, 0], (dpy, z)),
+            (rc.at[s, 3, 2:4], ra.at[s, 1], (dpx, z)),
+        )[kk]
+        return remote(src, dst, s1.at[s, kk], q1.at[s, kk], who)
+
+    def straight(s, kk):
+        src, dst, who = (
+            (rc.at[s, 1, 2:4], rb.at[s, 0, 2:4], (dpx, z)),
+            (rc.at[s, 2, 0:2], rb.at[s, 1, 0:2], (dpy, z)),
+            (rc.at[s, 1, 0:2], rb.at[s, 0, 0:2], (dpx, z)),
+            (rc.at[s, 2, 2:4], rb.at[s, 1, 2:4], (dpy, z)),
+        )[kk]
+        return remote(src, dst, s2.at[s, kk], q2.at[s, kk], who)
+
+    def last(s, d):
+        zz = (z + d) % T
+        return remote(rc.at[s, 0, zz], rz.at[s, d - 1], s3.at[s, d - 1], q3.at[s, d - 1], (dp, zz))
+
+    def add(dst, src):
+        @pl.loop(0, dst.shape[0])
+        def _(t):
+            dst[t] = (dst[t].astype(F32) + src[t].astype(F32)).astype(BF)
+
+    def sum_start(s):
+        for kk in (3, 1, 2, 0):
+            core_copy(s, kk).start()
+
+    def sum_core(s):
+        for kk in (3, 1, 2, 0):
+            core_copy(s, kk).wait_recv()
+            add(rc.at[s, kk], grad(s).at[:, rowsof(rel[kk]), :])
+            if kk == 3:
+                turn(s, 0).start()
+                turn(s, 1).start()
+            if kk == 1:
+                straight(s, 0).start()
+            if kk == 2:
+                straight(s, 1).start()
+
+    def sum_turn(s):
+        turn(s, 0).wait_recv()
+        add(rc.at[s, 1, 0:2], ra.at[s, 0])
+        straight(s, 2).start()
+        turn(s, 1).wait_recv()
+        add(rc.at[s, 2, 2:4], ra.at[s, 1])
+        straight(s, 3).start()
+
+    def sum_straight(s):
+        for kk in range(4):
+            straight(s, kk).wait_recv()
+        add(rc.at[s, 0], rb.at[s, 0])
+        add(rc.at[s, 0], rb.at[s, 1])
+        for d in range(1, T):
+            last(s, d).start()
+
+    def sum_last(s):
+        total = rc[s, 0, z].astype(F32)
+        for d in range(1, T):
+            last(s, d).wait_recv()
+            total = total + rz[s, d - 1].astype(F32)
+        if s == 0:
+            DQ[...] = total[:, 0:W]
+            DK[...] = total[:, W:2 * W]
+            DV[...] = total[:, 2 * W:3 * W]
+            DO[...] = total[:, 3 * W:4 * W].T
+        if s == 1:
+            D1[...] = total
+        if s == 2:
+            D2[...] = total.T
+
+    xT[:, 0:M] = low[...].T
+    xT[:, M:L] = flow[...].T
+
+    @pl.loop(0, T)
+    def _(t):
+        @pl.loop(0, M // RB)
+        def _(r):
+            rr = rows(r)
+            gi = (nn(low[rr, :], W_[2, t]) * gp[t, rr, :].astype(F32)).astype(BF)
+            gp[t, rr, :] = gi
+            SM[pl.ds(2 * T + t, 1), :] += colsum(gi.astype(F32))
+            gz[rr, :] += nt(gi, W_[1, t])
+
+        @pl.loop(0, D // RB)
+        def _(r):
+            W_[2, t, rows(r), :] = nn(xT[rows(r), 0:M], hid[t]).astype(BF)
+            W_[1, t, rows(r), :] = nn(xT[rows(r), M:L], gp[t]).astype(BF)
+
+    sum_start(2)
+    sum_start(1)
+
+    @pl.loop(0, M // RB)
+    def _(r):
+        rr = rows(r)
+        gf = gz[rr, :]
+        n = n1[rr, :]
+        g = gf * NP[1:2, :]
+        g1 = r1[rr, 0:1] * (g - mean_last(g) - n * mean_last(g * n))
+        SM[14:15, :] += colsum(gf * n)
+        SM[15:16, :] += colsum(gf)
+        SM[12:13, :] += colsum(g1)
+        gz[rr, :] = g1
+        low[rr, :] = g1.astype(BF)
+
+    xT[:, 0:M] = low[...].T
+
+    @pl.loop(0, T)
+    def _(t):
+        @pl.loop(0, M // RB)
+        def _(r):
+            hid[t, rows(r), 0:W] = nn(low[rows(r), :], W_[0, t, :, 3 * W:4 * W]).astype(BF)
+
+        @pl.loop(0, D // RB)
+        def _(r):
+            G0[t, rows(r), 3 * W:4 * W] = nn(xT[rows(r), 0:M], mixed[t, :, 0:W]).astype(BF)
+
+    @pl.loop(0, T)
+    def _(t):
+        @pl.when(t == 0)
+        def _():
+            sum_core(2)
+
+        @pl.when(t == 1)
+        def _():
+            sum_core(1)
+
+        @pl.when(t == 2)
+        def _():
+            sum_turn(2)
+            hand_on(outb, OF, orcv, 0)
+
+        @pl.when(t == 3)
+        def _():
+            sum_turn(1)
+
+        vT[...] = k[t, :, 0:W].T
+        for pair in range((NH + 1) // 2):
+            heads = [j for j in (2 * pair, 2 * pair + 1) if j < NH]
+            wide = HD * len(heads)
+            dk = jnp.zeros((L, wide), F32)
+            dv = jnp.zeros((L, wide), F32)
+            for j in heads:
+                for i in range(M // QC):
+                    qs = slice(i * QC, (i + 1) * QC)
+                    qm = only(head(q, t, qs, j), j)
+                    om = only(head(hid, t, qs, j), j)
+                    s = nt(head(k, t, everything, j), qm) + bias[:, qs]
+                    p = jnp.exp(s - lse[t * 4 + j, 0:1, qs])
+                    dpr = nt(head(v, t, everything, j), om)
+                    cen = jnp.sum(p * dpr, axis=0, keepdims=True)
+                    ds = (p * (dpr - cen)).astype(BF)
+                    dv = dv + nn(p.astype(BF), om)
+                    dk = dk + nn(ds, qm)
+                    oT[j * HD:(j + 1) * HD, qs] = nn(vT[j * HD:(j + 1) * HD, :], ds) * scale
+            lanes = slice(pair * 128, pair * 128 + wide)
+            k[t, :, lanes] = dk.astype(BF)
+            v[t, :, lanes] = dv.astype(BF)
+        dq = oT[...].T.astype(BF)
+        q[t, :, 0:W] = dq
+        SM[pl.ds(t, 1), 0:W] += colsum(dq.astype(F32))
+        SM[pl.ds(T + t, 1), 0:W] += colsum(v[t, :, 0:W].astype(F32))
+
+    @pl.loop(0, M // RB)
+    def _(r):
+        acc = jnp.zeros((RB, D), F32)
+        for t in range(T):
+            acc = acc + nt(k[t, othrows(r), 0:W], W_[0, t, :, W:2 * W])
+            acc = acc + nt(v[t, othrows(r), 0:W], W_[0, t, :, 2 * W:3 * W])
+        flow[rows(r), :] = acc.astype(BF)
+
+    part = remote(flow, rgt, gs, gr, (dpc, z))
+    part.start()
+
+    @pl.loop(0, M // RB)
+    def _(r):
+        acc = gz[rows(r), :]
+        for t in range(T):
+            acc = acc + nt(q[t, rows(r), 0:W], W_[0, t, :, 0:W])
+            acc = acc + nt(k[t, ownrows(r), 0:W], W_[0, t, :, W:2 * W])
+            acc = acc + nt(v[t, ownrows(r), 0:W], W_[0, t, :, 2 * W:3 * W])
+        gz[rows(r), :] = acc
+
+    part.wait_recv()
+    low[...] = (gz[...] + rgt[...].astype(F32)).astype(BF)
+    push(low, GF, gsem, grcv, gsl)
+
+    pals = [(dpc, z), (dpx, z), (dpy, z), (dp, z + 1 - 2 * (z % 2)), (dp, (z + 2) % T)]
+
+    def small(step):
+        return remote(ssend.at[step], srecv.at[step], ms.at[step], mr.at[step], pals[step])
+
+    def small_start(step):
+        ssend[step] = SM[...]
+        small(step).start()
+
+    def small_end(step):
+        small(step).wait_recv()
+        SM[...] += srecv[step]
+
+    small_start(0)
+    sum_straight(2)
+
+    xT[...] = X[...].T
+
+    @pl.loop(0, T)
+    def _(t):
+        @pl.loop(0, D // RB)
+        def _(r):
+            rr = rows(r)
+            G0[t, rr, 0:W] = nn(xT[rr, pl.ds(pl.multiple_of(own, 128), M)], q[t, :, 0:W]).astype(BF)
+            G0[t, rr, W:2 * W] = nn(xT[rr, :], k[t, :, 0:W]).astype(BF)
+            G0[t, rr, 2 * W:3 * W] = nn(xT[rr, :], v[t, :, 0:W]).astype(BF)
+
+    sum_start(0)
+    small_end(0)
+    small_start(1)
+    sum_straight(1)
+    sum_core(0)
+    small_end(1)
+    small_start(2)
+    sum_last(2)
+    sum_turn(0)
+    small_end(2)
+    small_start(3)
+    sum_last(1)
+    small_end(3)
+    small_start(4)
+    hand_on(low, GF, grcv, 2)
+    small_end(4)
+    sum_straight(0)
+    sum_last(0)
+
+    BQ[...] = SM[pl.ds(z, 1), 0:W]
+    BV[...] = SM[pl.ds(T + z, 1), 0:W]
+    B1[...] = SM[pl.ds(2 * T + z, 1), :]
+    VEC[...] = SM[3 * T:3 * T + 8, :]
+    settle(outb, OF, orcv, 0)
+    settle(low, GF, grcv, 2)
+    pushed(outb, OF, osem, orcv, osl)
+    pushed(low, GF, gsem, grcv, gsl)
+    part.wait_send()
+    for step in range(5):
+        small(step).wait_send()
+    for s in range(SL):
+        for kk in range(4):
+            core_copy(s, kk).wait_send()
+            straight(s, kk).wait_send()
+        turn(s, 0).wait_send()
+        turn(s, 1).wait_send()
+        for d in range(1, T):
+            last(s, d).wait_send()
+
+
+def layer_call(wq, wk, wv, wo, w1, w2t, norms, biases, lengths, tokens, cotangent, T):
+    S, W = wq.shape
+    D = tokens.shape[1]
+    F = w1.shape[1]
+    L = tokens.shape[0] // lengths.shape[0]
+    M = L // 2
+    SL = 3
+    WP = 256
+    any_ = pl.BlockSpec(memory_space=pl.ANY)
+    vm = pl.BlockSpec(memory_space=pltpu.VMEM)
+    dma = pltpu.SemaphoreType.DMA
+    f32 = lambda *s: jax.ShapeDtypeStruct(s, F32)
+    V = pltpu.VMEM
+    return pl.pallas_call(
+        layer_kernel,
+        in_specs=[vm] * 8 + [pl.BlockSpec(memory_space=pltpu.SMEM), any_, any_],
+        out_specs=[any_, any_] + [vm] * 10,
+        out_shape=[
+            jax.ShapeDtypeStruct((4 * M, D), BF),
+            jax.ShapeDtypeStruct((4 * M, D), BF),
+            f32(S, W), f32(S, W), f32(S, W), f32(W, S), f32(S, F), f32(F, S),
+            f32(1, W), f32(1, W), f32(1, F), f32(8, D),
+        ],
+        scratch_shapes=[
+            V((SL, S, D), BF),
+            V((SL, T, D, F), BF),
+            V((T, D, D), BF),
+            V((L, D), BF),
+            V((M, D), BF),
+            V((2, 8, L), F32),
+            V((T, 8, D), F32),
+            V((24, D), F32),
+            V((T, M, WP), BF),
+            V((T, L, WP), BF),
+            V((T, L, WP), BF),
+            V((T, M, WP), BF),
+            V((W, L), BF),
+            V((W, M), F32),
+            V((T * 4, 8, M), F32),
+            V((L, M), F32),
+            V((M, D), F32),
+            V((M, 128), F32),
+            V((M, D), BF),
+            V((T, M, F), BF),
+            V((T, M, F), BF),
+            V((M, D), F32),
+            V((M, D), BF),
+            V((D, L), BF),
+            V((M, D), BF),
+            V((M, D), BF),
+            V((SL, 4, T, S, D), BF),
+            V((SL, 2, 2, S, D), BF),
+            V((SL, 2, T, S, D), BF),
+            V((SL, T - 1, S, D), BF),
+            V((5, 24, D), F32),
+            V((5, 24, D), F32),
+            dma((2,)),
+            dma((SL, T - 1)), dma((SL, T - 1)),
+            dma((3, SL, T)), dma((SL, T)), dma((SL, T)), dma((4, SL, T)),
+            dma((SL, T)), dma((SL, T)),
+            dma((3, SL, T)),
+            dma((T - 1,)), dma((T - 1,)),
+            dma((3,)), dma((3,)),
+            dma, dma,
+            dma((5,)), dma((4,)), dma,
+            dma((5,)), dma((4,)), dma,
+            dma((4,)),
+            dma((SL, 4)), dma((SL, 4)),
+            dma((SL, 2)), dma((SL, 2)),
+            dma((SL, 4)), dma((SL, 4)),
+            dma((SL, T - 1)), dma((SL, T - 1)),
+            dma((5,)), dma((5,)),
+        ],
+        compiler_params=pltpu.CompilerParams(
+            collective_id=0, has_side_effects=True, vmem_limit_bytes=64 << 20
+        ),
+    )(wq, wk, wv, wo, w1, w2t, norms, biases, lengths, tokens, cotangent)
 
 
 def doc_ids(lengths, count):
@@ -67,7 +815,7 @@
 
 def norm_forward(total, gain, shift):
     centre = total - jnp.mean(total, axis=-1, keepdims=True)
-    scaled = lax.rsqrt(jnp.mean(centre * centre, axis=-1, keepdims=True) + eps_norm)
+    scaled = lax.rsqrt(jnp.mean(centre * centre, axis=-1, keepdims=True) + EPS)
     normed = centre * scaled
     return (normed * gain + shift, normed, scaled)
 
@@ -86,10 +834,10 @@
         * scale
     )
     same_doc = seg_block[:, None] == seg[None, :]
-    return jnp.where(same_doc[None], raw, masked_score)
-
-
-def body(
+    return jnp.where(same_doc[None], raw, NEG)
+
+
+def general_body(
     tokens,
     doc_lengths,
     wq,
@@ -307,6 +1055,20 @@
     )
 
 
+def split_body(T, tokens, doc_lengths, wq, bq, wk, wv, bv, wo, bo, gain1, shift1, w1, b1, w2, b2,
+               gain2, shift2, cotangent):
+    S, W = wq.shape
+    D = tokens.shape[1]
+    F = w1.shape[1]
+    row = lambda x: jnp.pad(x[None, :], ((0, 0), (0, D - x.shape[0])))
+    biases = jnp.concatenate([row(b1), row(bq), row(bv), jnp.zeros((5, D), F32)])
+    norms = jnp.stack([bo, gain1, shift1, b2, gain2, shift2, bo, bo])
+    (full, grads, dq, dk, dv, do, d1, d2, gbq, gbv, gb1, vec) = layer_call(
+        wq, wk, wv, wo, w1, w2.T, norms, biases, doc_lengths, tokens, cotangent, T)
+    return (full, grads, dq, gbq[0], dk, dv, gbv[0], do, vec[0], vec[2], vec[3], d1, gb1[0], d2,
+            vec[1], vec[4], vec[5])
+
+
 def solution(mesh):
     placed = (
         P("dp", None),
@@ -328,6 +1090,10 @@
         P(),
         P("dp", None),
     )
+    if mesh.shape["dp"] == 8 and mesh.shape["tensor"] == 4:
+        body = partial(split_body, mesh.shape["tensor"])
+    else:
+        body = general_body
     return jax.shard_map(
         body,
         mesh=mesh,

time: 850 us -> 280 us (0.33)
  waiting for transfers between devices: 509 us -> 0 us
  Pallas kernels: 0 us -> 257 us
  matrix products: 153 us -> 0 us
  other arithmetic: 75.5 us -> 2.65 us
  blocking collectives: 63.1 us -> 0 us
  between operations: 17.4 us -> 0.72 us
    psum x4 -> x0, waiting for transfers between devices: 416 us -> none  [the longest x1 121 us: body(): lax.psum(jnp.dot(hidden, full_second, preferred_element_type=jnp.float32)...]
    pallas_call x0 -> x1, Pallas kernels: none -> 257 us  [layer_call(): pl.pallas_call(layer_kernel, in_specs=[vm] * 8 + [pl.BlockSpec(memory_spa...]
    dot_general x60 -> x0, matrix products: 153 us -> none  [the longest x12 21.3 us: contract_cols(): lax.dot_general(left, right, (((1,), (1,)), ((), ())), preferred_element_...]
    unnamed x16 -> x0, waiting for transfers between devices: 92.8 us -> none
    all_gather x4 -> x0, blocking collectives: 39.1 us -> none  [the longest x1 11.4 us: collect(): lax.all_gather(wv, 'dp', axis=0, tiled=True)]
    reduce_sum x17 -> x0, other arithmetic: 38 us -> none  [the longest x1 9.65 us: norm_backward(): jnp.sum(grad_result * normed, axis=0)]
    psum x1 -> x0, blocking collectives: 24 us -> none  [reduce_small(): lax.psum((grads[0], grads[1], grads[2], grads[3], grads[4], grads[5], gra...]
    convert_element_type x4 -> x0, other arithmetic: 19.8 us -> none  [the longest x2 16.6 us: body(): grad_scores = (probs * (grad_probs - centre)).astype(jnp.bfloat16)]
  transfers between devices with their start and end apart: 12 -> 0, of which waited for: 7 -> 0; matrix products, arithmetic and copies ran while one was open for 11% -> 0% of each run, Pallas kernels for 0% -> 0%
where the time goes in v2:
time: 280 us; the launch traced here: 279 us
  Pallas kernels  257 us (92%)
  local copies, waits for them, and re-layouts  19 us (7%)
    pallas_call x1, Pallas kernels, layer_call(): pl.pallas_call(layer_kernel, in_specs=[vm] * 8 + [pl.BlockSpec(memory_spa...  257 us
    unnamed x26, local copies, waits for them, and re-layouts  11.9 us

profile of v2, /device:TPU:1, one launch (start us, length us, event | category | flops | bytes accessed | tf_op | source)
XLA Modules:
  0.0 279.4 jit_solution(8168015140004075503)
XLA Ops:
  0.7 0.1 pad.12.clone
  0.7 0.7 stack.23
  1.4 0.7 stack.24
  2.1 0.7 stack.25
  2.8 0.7 broadcast_in_dim.12
  3.5 0.7 stack.26
  4.2 0.7 stack.27
  4.9 0.7 stack.28
  5.6 0.6 stack.29.NP
  6.2 1.4 fusion.BP
  7.6 256.9 %shard_map.305 = (bf16[2048,768]{1,0:T(8,128)(2,1)}, bf16[2048,768]{1,0:T(8,128)(2,1)}, f32[96,192]{1,0:T(8,128)}, f32[96,192]{1,0:T(8,128)}, f32[96,192]{1,0:T(...) custom-call(bf16[96,192]{1,0:T(8,128)(2,1)} %WQ.1, ...), custom_call_target="tpu_custom_call" | custom-call | tf_op jit(solution)/shard_map/pallas_call | solution.py:697
  264.5 1.3 reduce.3
  265.8 1.6 slice_reduce_fusion
  267.4 1.9 copy.35
  269.3 3.9 %copy.45 = bf16[2048,768]{1,0:T(8,128)(2,1)} copy(bf16[2048,768]{1,0:T(8,128)(2,1)} %get-tuple-element.81) | data formatting | bytes 6291456
  273.3 1.7 copy.46
  274.9 0.0 copy-done.5
  274.9 0.6 copy.47
  275.6 0.6 copy.48
  276.1 0.6 copy.49
  276.8 0.6 copy.50
  277.4 0.6 copy.51
  278.0 0.6 copy.52
  278.6 0.7 copy.53
  (16 shorter events, 0.0 us)
Async XLA Ops:
  269.3 3.9 %copy-start = (bf16[2048,768]{1,0:T(8,128)(2,1)S(1)}, bf16[2048,768]{1,0:T(8,128)(2,1)}, u32[]{:S(2)}) copy-start(bf16[2048,768]{1,0:T(8,128)(2,1)} %get-tuple-element.82) | copy-start | bytes 9437188
  273.2 1.7 copy-start.5
  273.2 2.4 copy-start.7
  273.2 2.9 %copy-start.4 = (f32[96,192]{1,0:T(8,128)S(1)}, f32[96,192]{1,0:T(8,128)}, u32[]{:S(2)}) copy-start(f32[96,192]{1,0:T(8,128)} %get-tuple-element.85) | copy-start | bytes 221188
  273.2 3.6 %copy-start.3 = (f32[96,192]{1,0:T(8,128)S(1)}, f32[96,192]{1,0:T(8,128)}, u32[]{:S(2)}) copy-start(f32[96,192]{1,0:T(8,128)} %get-tuple-element.86) | copy-start | bytes 221188
  273.2 4.2 %copy-start.6 = (f32[1,192]{1,0:T(1,128)S(1)}, f32[1,192]{1,0:T(1,128)}, u32[]{:S(2)}) copy-start(f32[1,192]{1,0:T(1,128)} %get-tuple-element.35) | copy-start | bytes 2308
  273.2 4.8 %copy-start.2 = (f32[192,96]{1,0:T(8,128)S(1)}, f32[192,96]{1,0:T(8,128)}, u32[]{:S(2)}) copy-start(f32[192,96]{1,0:T(8,128)} %get-tuple-element.88) | copy-start | bytes 221188
  273.2 5.4 %copy-start.1 = (f32[96,768]{1,0:T(8,128)S(1)}, f32[96,768]{1,0:T(8,128)}, u32[]{:S(2)}) copy-start(f32[96,768]{1,0:T(8,128)} %get-tuple-element.92) | copy-start | bytes 884740

commit v3 on v2

--- a/solution.py
+++ b/solution.py
@@ -45,12 +45,12 @@
 
 
 def layer_kernel(
-    WQ, WK, WV, WO, W1, W2T, NP, BP, LEN, TOK, COT,
-    OF, GF, DQ, DK, DV, DO, D1, D2, BQ, BV, B1, VEC,
-    PK, W_, G0, X, CO, SG, BI, SM,
-    q, k, v, mixed, vT, oT, lse, bias, n1, r1, flow, hid, gp, gz, low, xT, outb,
+    WQ, WK, WV, WO, W1, W2T, BO_, GAIN1, SHIFT1, B2_, GAIN2, SHIFT2, B1_, BQ_, BV_, LEN, TOK, COT,
+    OF, GF, GR, SMO,
+    PK, W_, X, CO, SG, NP, BP, BI, SM,
+    q, k, v, mixed, vT, oT, lse, bias, n1, r1, flow, hid, gp, gz, low, xT,
     rgt, rc, ra, rb, rz, ssend, srecv,
-    loc, zs, zr, os_, xr, yr, cr, fs, dr, ks, bs, br, ts, tr,
+    loc, zs, zf, zr, os_, xr, yr, cr, fs, dr, ks, bs, br, ts, tr,
     gs, gr, osem, orcv, osl, gsem, grcv, gsl, fwd, cs, crr, s1, q1, s2, q2, s3, q3, ms, mr,
 ):
     SL, S, D = PK.shape
@@ -80,12 +80,20 @@
     def othrows(r):
         return pl.ds(pl.multiple_of(oth + r * RB, RB), RB)
 
+    ownhalf = pl.ds(pl.multiple_of(own, M), M)
+    othhalf = pl.ds(pl.multiple_of(oth, M), M)
+
     PK[0, :, 0:W] = WQ[...]
     PK[0, :, W:2 * W] = WK[...]
     PK[0, :, 2 * W:3 * W] = WV[...]
     PK[0, :, 3 * W:4 * W] = WO[...].T
     PK[1] = W1[...]
     PK[2] = W2T[...]
+    for i, ref in enumerate((BO_, GAIN1, SHIFT1, B2_, GAIN2, SHIFT2)):
+        NP[i:i + 1, :] = ref[...].reshape(1, D)
+    BP[0:1, :] = B1_[...].reshape(1, D)
+    BP[1:2, 0:W] = BQ_[...].reshape(1, W)
+    BP[2:3, 0:W] = BV_[...].reshape(1, W)
 
     spot = lax.broadcasted_iota(jnp.int32, (8, L), 1)
     doc = jnp.zeros((8, L), F32)
@@ -105,12 +113,33 @@
     def block(s, t, i):
         return W_.at[s, t, pl.ds(pl.multiple_of(i * S, S), S), :]
 
+    half = z // 2
+
     def source(d):
-        return (z - d + T) % T
+        edge = z + half * (3 - 2 * z)
+        swap = edge * (1 - d // 2)
+        t = swap * (1 - d) + (1 - swap) * d
+        return t + half * (3 - 2 * t)
+
+    right, left = (dp, (z + 1) % T), (dp, (z + T - 1) % T)
+    can_right, can_left = z < T - 1, z > 0
+
+    def send_z(s):
+        return (
+            (can_right, remote(PK.at[s], block(s, z, dp), zs.at[s, 0], zr.at[s, z], right)),
+            (can_left, remote(PK.at[s], block(s, z, dp), zs.at[s, 1], zr.at[s, z], left)),
+        )
+
+    def pass_z(s, t):
+        here = block(s, t, dp)
+        return (
+            (can_right & (t < z), remote(here, here, zf.at[s, t], zr.at[s, t], right)),
+            (can_left & (t > z), remote(here, here, zf.at[s, t], zr.at[s, t], left)),
+        )
 
     def push_z(s):
-        for d in range(1, T):
-            remote(PK.at[s], block(s, z, dp), zs.at[s, d - 1], zr.at[s, d - 1], (dp, (z + d) % T)).start()
+        for able, copy in send_z(s):
+            pl.when(able)(copy.start)
 
     def send_block(s, d, src):
         t = source(d)
@@ -122,8 +151,12 @@
         t = source(d)
         remote(block(s, t, i), block(s, t, i), ks.at[kind - 1, s, d], cr.at[kind, s, d], (dpc, z)).start()
 
-    def wait_z(s, d):
-        remote(PK.at[s], block(s, source(d), dp), zs.at[s, d - 1], zr.at[s, d - 1], (dp, (z + 1) % T)).wait_recv()
+    def take_z(s, d):
+        t = source(d)
+        remote(PK.at[s], block(s, t, dp), zs.at[s, 0], zr.at[s, t], right).wait_recv()
+        for able, copy in pass_z(s, t):
+            pl.when(able)(copy.start)
+        send_block(s, d, block(s, t, dp))
 
     def take_x(s, d):
         t = source(d)
@@ -150,6 +183,9 @@
         pass_core(3, s, d, dpxy)
 
     PIECES = SL * T
+    XL, DL = 2, 4
+    STEPS = PIECES + DL
+    first_steps = DL + 1
 
     def gather_step(n):
         n = jnp.int32(n)
@@ -160,28 +196,27 @@
 
             @pl.when(d > 0)
             def _():
-                wait_z(s, d)
-                send_block(s, d, block(s, source(d), dp))
-
-            @pl.when((d == T - 1) & (s + 1 < SL))
+                take_z(s, d)
+
+            @pl.when(d == 0)
             def _():
-                push_z(s + 1)
-
-        @pl.when((n >= 1) & (n <= PIECES))
+                send_block(s, d, PK.at[s])
+
+        @pl.when((n >= XL) & (n < PIECES + XL))
         def _():
-            take_x((n - 1) // T, (n - 1) % T)
-            take_y((n - 1) // T, (n - 1) % T)
-
-        @pl.when((n >= 3) & (n < PIECES + 3))
+            take_x((n - XL) // T, (n - XL) % T)
+            take_y((n - XL) // T, (n - XL) % T)
+
+        @pl.when((n >= DL) & (n < PIECES + DL))
         def _():
-            take_diag((n - 3) // T, (n - 3) % T)
-
-    def gathered(s):
-        for d in range(T):
-            for kind, i in enumerate((dpc, dpx + flip, dpy + flip, dpxy + flip)):
-                remote(PK.at[s], block(s, source(d), i), os_.at[2, s, d], cr.at[kind, s, d], (dpc, z)).wait_recv()
-
-    push_z(0)
+            take_diag((n - DL) // T, (n - DL) % T)
+
+    def gathered(s, d):
+        for kind, i in enumerate((dpc, dpx + flip, dpy + flip, dpxy + flip)):
+            remote(PK.at[s], block(s, source(d), i), os_.at[2, s, d], cr.at[kind, s, d], (dpc, z)).wait_recv()
+
+    for s in range(SL):
+        push_z(s)
     seq = pl.ds(pl.multiple_of((z % 2) * L, L), L)
     mine = pl.ds(pl.multiple_of((z % 2) * L + own, M), M)
     other = pl.ds(pl.multiple_of((z % 2) * L + oth, M), M)
@@ -199,12 +234,11 @@
     for d in range(1, T):
         remote(BP, BI.at[z], bs.at[d - 1], br.at[d - 1], (dp, (z + d) % T)).start()
     for s in range(SL):
-        send_block(s, 0, PK.at[s])
         W_[s, z, pl.ds(pl.multiple_of(dp * S, S), S), :] = PK[s]
     BI[z] = BP[...]
     SM[...] = jnp.zeros_like(SM)
 
-    @pl.loop(0, T + 1)
+    @pl.loop(0, 2)
     def _(n):
         gather_step(n)
 
@@ -221,7 +255,7 @@
             copy.wait_recv()
 
     for d in range(1, T):
-        remote(BP, BI.at[source(d)], bs.at[d - 1], br.at[d - 1], (dp, (z + 1) % T)).wait_recv()
+        remote(BP, BI.at[(z - d + T) % T], bs.at[d - 1], br.at[d - 1], (dp, (z + 1) % T)).wait_recv()
 
     docs = jnp.where(core == home, SG[0], SG[1])
     SG[0] = docs
@@ -230,26 +264,22 @@
         query_doc = SG[0, 0:1, pl.ds(pl.multiple_of(own + i * 128, 128), 128)]
         bias[:, i * 128:(i + 1) * 128] = jnp.where(key_doc == query_doc, 0.0, NEG)
 
-    @pl.loop(T + 1, T + 3)
+    @pl.loop(2, first_steps)
     def _(n):
         gather_step(n)
 
-    gathered(0)
-
     @pl.loop(0, T)
-    def _(t):
-        @pl.loop(0, L // RB)
-        def _(r):
-            xs = X[rows(r), :]
-            k[t, rows(r), 0:W] = nn(xs, W_[0, t, :, W:2 * W]).astype(BF)
-            v[t, rows(r), 0:W] = (nn(xs, W_[0, t, :, 2 * W:3 * W]) + BI[t, 2:3, 0:W]).astype(BF)
-
-        @pl.loop(0, M // RB)
-        def _(r):
-            xs = X[ownrows(r), :]
-            q[t, rows(r), 0:W] = (
-                (nn(xs, W_[0, t, :, 0:W]) + BI[t, 1:2, 0:W]).astype(BF) * BF(scale)
-            ).astype(BF)
+    def _(d):
+        gather_step(first_steps + d)
+        gathered(0, d)
+        t = source(d)
+        mine_qkv = nn(X[ownhalf, :], W_[0, t, :, 0:3 * W])
+        q[t, :, 0:W] = ((mine_qkv[:, 0:W] + BI[t, 1:2, 0:W]).astype(BF) * BF(scale)).astype(BF)
+        k[t, ownhalf, 0:W] = mine_qkv[:, W:2 * W].astype(BF)
+        v[t, ownhalf, 0:W] = (mine_qkv[:, 2 * W:3 * W] + BI[t, 2:3, 0:W]).astype(BF)
+        their_kv = nn(X[othhalf, :], W_[0, t, :, W:3 * W])
+        k[t, othhalf, 0:W] = their_kv[:, 0:W].astype(BF)
+        v[t, othhalf, 0:W] = (their_kv[:, W:2 * W] + BI[t, 2:3, 0:W]).astype(BF)
 
     lane = lax.broadcasted_iota(jnp.int32, (1, 128), 1)
 
@@ -269,12 +299,11 @@
 
     @pl.loop(0, T)
     def _(t):
-        gather_step(T + 3 + t)
+        gather_step(first_steps + T + t)
         vT[...] = v[t, :, 0:W].T
 
-        @pl.loop(0, M // QC)
-        def _(i):
-            qs = rows(i, QC)
+        for i in range(M // QC):
+            qs = slice(i * QC, (i + 1) * QC)
             for j in range(NH):
                 s = nt(head(k, t, everything, j), only(head(q, t, qs, j), j)) + bias[:, qs]
                 m = jnp.max(s, axis=0, keepdims=True)
@@ -298,36 +327,33 @@
         r1[rows(r), :] = jnp.broadcast_to(rs, (RB, 128))
         flow[rows(r), :] = (n * NP[1:2, :] + NP[2:3, :]).astype(BF)
 
-    gather_step(2 * T + 3)
-    gathered(1)
-
     @pl.loop(0, T)
-    def _(t):
-        @pl.when(t < T - 1)
-        def _():
-            gather_step(2 * T + 4 + t)
-
-        @pl.loop(0, M // RB)
-        def _(r):
-            rr = rows(r)
-            inner = nn(flow[rr, :], W_[1, t]) + BI[t, 0:1, :]
-            phi = 0.5 * (1.0 + lax.erf(inner * (2.0 ** -0.5)))
-            hid[t, rr, :] = (inner * phi).astype(BF)
-            gp[t, rr, :] = (phi + inner * (jnp.exp(-0.5 * inner * inner) * 0.3989422804014327)).astype(BF)
-
-    gathered(2)
+    def _(d):
+        gather_step(first_steps + 2 * T + d)
+        gathered(1, d)
+        t = source(d)
+        inner = nn(flow[...], W_[1, t]) + BI[t, 0:1, :]
+        phi = 0.5 * (1.0 + lax.erf(inner * (2.0 ** -0.5)))
+        hid[t] = (inner * phi).astype(BF)
+        gp[t] = (phi + inner * (jnp.exp(-0.5 * inner * inner) * 0.3989422804014327)).astype(BF)
+
+    gz[...] = n1[...] * NP[1:2, :] + NP[2:3, :] + NP[3:4, :]
+
+    @pl.loop(0, T)
+    def _(d):
+        gathered(2, d)
+        t = source(d)
+        gz[...] += nt(hid[t], W_[2, t])
 
     @pl.loop(0, M // RB)
     def _(r):
         rr = rows(r)
-        zz = n1[rr, :] * NP[1:2, :] + NP[2:3, :] + NP[3:4, :]
-        for t in range(T):
-            zz = zz + nt(hid[t, rr, :], W_[2, t])
+        zz = gz[rr, :]
         cen = zz - mean_last(zz)
         rs = lax.rsqrt(mean_last(cen * cen) + EPS)
         n = cen * rs
-        outb[rr, :] = (n * NP[4:5, :] + NP[5:6, :]).astype(BF)
         ct = CO[rr, :].astype(F32)
+        CO[rr, :] = (n * NP[4:5, :] + NP[5:6, :]).astype(BF)
         g = ct * NP[4:5, :]
         g2 = rs * (g - mean_last(g) - n * mean_last(g * n))
         SM[16:17, :] += colsum(ct * n)
@@ -342,71 +368,76 @@
         return pl.ds(pl.multiple_of(((zz % 2) * 2 + cc) * M, M), M)
 
     def pushes(src, full, sems, recv):
-        copies = []
-        for d in (2, 1):
-            for sign in (1, -1):
-                zz = z + sign * d
-                copies.append((zz, remote(
-                    src, full.at[spotrows(z, core)], sems.at[(d - 1) * 2 + (sign < 0)],
-                    recv.at[(z % 2) * 2 + core], (dest, (zz + T) % T))))
-        return copies
+        return [
+            (able, remote(src, full.at[spotrows(z, core)], sems.at[i], recv.at[(z % 2) * 2 + core], (dest, chip)))
+            for i, (able, chip) in enumerate(((can_right, (z + 1) % T), (can_left, (z + T - 1) % T)))
+        ]
 
     def own_copy(src, full, sems, recv, slot):
-        away = remote(src, full.at[spotrows(z, core)], sems.at[4], recv.at[(z % 2) * 2 + core], (dpc, z))
+        away = remote(src, full.at[spotrows(z, core)], sems.at[2], recv.at[(z % 2) * 2 + core], (dpc, z))
         here = pltpu.make_async_copy(src, full.at[spotrows(z, core)], slot)
         return away, here
 
     def push(src, full, sems, recv, slot):
-        for zz, copy in pushes(src, full, sems, recv):
-            pl.when((zz >= 0) & (zz < T))(copy.start)
+        for able, copy in pushes(src, full, sems, recv):
+            pl.when(able)(copy.start)
         away, here = own_copy(src, full, sems, recv, slot)
         pl.when(core != home)(away.start)
         pl.when(core == home)(here.start)
 
     def pushed(src, full, sems, recv, slot):
-        for zz, copy in pushes(src, full, sems, recv):
-            pl.when((zz >= 0) & (zz < T))(copy.wait_send)
+        for able, copy in pushes(src, full, sems, recv):
+            pl.when(able)(copy.wait_send)
         away, here = own_copy(src, full, sems, recv, slot)
         pl.when(core != home)(away.wait_send)
         pl.when(core == home)(here.wait)
 
-    relay = ((core == 0) & (z == 2)) | ((core == 1) & (z == 1))
-    far = 3 * core
-    beyond = 3 - far
-
-    def got(src, full, recv, zz, cc):
-        remote(src, full.at[spotrows(zz, cc)], gs, recv.at[(zz % 2) * 2 + cc], (dpx, z)).wait_recv()
-
-    def handing(full, recv, base, cc):
-        return remote(full.at[spotrows(far, cc)], full.at[spotrows(far, cc)], fwd.at[base + cc],
-                      recv.at[(far % 2) * 2 + cc], (dp, beyond))
-
-    def hand_on(src, full, recv, base):
-        @pl.when(relay)
+    ahead = 1 - 2 * core
+
+    def moves(hop):
+        if hop == 0:
+            return (z == 1) | (z == 2)
+        return z == 2 - core
+
+    def got(src, full, recv, b, cc):
+        remote(src, full.at[spotrows(b, cc)], gs, recv.at[(b % 2) * 2 + cc], (dpx, z)).wait_recv()
+
+    def handing(full, recv, base, hop, cc):
+        b = z - ahead * (hop + 1)
+        return remote(full.at[spotrows(b, cc)], full.at[spotrows(b, cc)], fwd.at[base + 2 * hop + cc],
+                      recv.at[(b % 2) * 2 + cc], (dp, (z + ahead) % T))
+
+    def hand_on(src, full, recv, base, hop):
+        @pl.when(moves(hop))
         def _():
             for cc in range(2):
-                got(src, full, recv, far, cc)
-                handing(full, recv, base, cc).start()
+                got(src, full, recv, z - ahead * (hop + 1), cc)
+                handing(full, recv, base, hop, cc).start()
 
     def settle(src, full, recv, base):
         for kk in range(2):
             for cc in range(2):
-                zz = core * 2 + kk
-
-                @pl.when(jnp.logical_not((zz == z) & (core == cc)) & jnp.logical_not(relay & (zz == far)))
+                b = core * 2 + kk
+                gone = (moves(0) & (b == z - ahead)) | (moves(1) & (b == z - 2 * ahead))
+
+                @pl.when(jnp.logical_not((b == z) & (core == cc)) & jnp.logical_not(gone))
                 def _():
-                    got(src, full, recv, zz, cc)
-
-        @pl.when(relay)
-        def _():
-            for cc in range(2):
-                handing(full, recv, base, cc).wait_send()
-
-    push(outb, OF, osem, orcv, osl)
+                    got(src, full, recv, b, cc)
+
+        for hop in range(2):
+            @pl.when(moves(hop))
+            def _():
+                for cc in range(2):
+                    handing(full, recv, base, hop, cc).wait_send()
+
+    push(CO, OF, osem, orcv, osl)
 
     for s in range(SL):
-        for d in range(1, T):
-            remote(PK.at[s], block(s, z, dp), zs.at[s, d - 1], zr.at[s, d - 1], (dp, (z + d) % T)).wait_send()
+        for able, copy in send_z(s):
+            pl.when(able)(copy.wait_send)
+        for t in range(T):
+            for able, copy in pass_z(s, t):
+                pl.when(able)(copy.wait_send)
         for d in range(T):
             for kind in range(3):
                 remote(PK.at[s], block(s, z, dp), os_.at[kind, s, d], xr.at[s, d], (dpx, z)).wait_send()
@@ -416,7 +447,7 @@
         remote(BP, BI.at[z], bs.at[d - 1], br.at[d - 1], (dp, (z + d) % T)).wait_send()
 
     def grad(s):
-        return G0 if s == 0 else W_.at[s]
+        return W_.at[s]
 
     rel = (dp, dpx, dpy, dpxy)
 
@@ -442,9 +473,9 @@
         )[kk]
         return remote(src, dst, s2.at[s, kk], q2.at[s, kk], who)
 
-    def last(s, d):
-        zz = (z + d) % T
-        return remote(rc.at[s, 0, zz], rz.at[s, d - 1], s3.at[s, d - 1], q3.at[s, d - 1], (dp, zz))
+    def along(s, t, sign):
+        way = (1 - sign) // 2
+        return remote(rc.at[s, 0, t], rz.at[s, way, t], s3.at[s, way, t], q3.at[s, way, t], (dp, (z + sign + T) % T))
 
     def add(dst, src):
         @pl.loop(0, dst.shape[0])
@@ -480,41 +511,51 @@
             straight(s, kk).wait_recv()
         add(rc.at[s, 0], rb.at[s, 0])
         add(rc.at[s, 0], rb.at[s, 1])
-        for d in range(1, T):
-            last(s, d).start()
+
+    def sum_along(s):
+        @pl.loop(0, 2)
+        def _(i):
+            sign = (1 - 2 * half) * (1 - 2 * i)
+            way = (1 - sign) // 2
+            behind = z - sign
+
+            @pl.loop(0, T - 1)
+            def _(j):
+                t = (1 - way) * (T - 1 - j) + way * j
+
+                @pl.when((t - z) * sign > 0)
+                def _():
+                    @pl.when((behind >= 0) & (behind < T))
+                    def _():
+                        along(s, t, sign).wait_recv()
+                        rc[s, 0, t] = (rc[s, 0, t].astype(F32) + rz[s, way, t].astype(F32)).astype(BF)
+
+                    along(s, t, sign).start()
 
     def sum_last(s):
-        total = rc[s, 0, z].astype(F32)
-        for d in range(1, T):
-            last(s, d).wait_recv()
-            total = total + rz[s, d - 1].astype(F32)
-        if s == 0:
-            DQ[...] = total[:, 0:W]
-            DK[...] = total[:, W:2 * W]
-            DV[...] = total[:, 2 * W:3 * W]
-            DO[...] = total[:, 3 * W:4 * W].T
-        if s == 1:
-            D1[...] = total
-        if s == 2:
-            D2[...] = total.T
+        GR[s] = rc[s, 0, z].astype(F32)
+        for sign in (1, -1):
+            @pl.when((z - sign >= 0) & (z - sign < T))
+            def _():
+                along(s, z, sign).wait_recv()
+                GR[s] += rz[s, (1 - sign) // 2, z].astype(F32)
+
+    def sum_sent(s):
+        for sign in (1, -1):
+            for t in range(T):
+                pl.when((t - z) * sign > 0)(along(s, t, sign).wait_send)
 
     xT[:, 0:M] = low[...].T
     xT[:, M:L] = flow[...].T
 
     @pl.loop(0, T)
     def _(t):
-        @pl.loop(0, M // RB)
-        def _(r):
-            rr = rows(r)
-            gi = (nn(low[rr, :], W_[2, t]) * gp[t, rr, :].astype(F32)).astype(BF)
-            gp[t, rr, :] = gi
-            SM[pl.ds(2 * T + t, 1), :] += colsum(gi.astype(F32))
-            gz[rr, :] += nt(gi, W_[1, t])
-
-        @pl.loop(0, D // RB)
-        def _(r):
-            W_[2, t, rows(r), :] = nn(xT[rows(r), 0:M], hid[t]).astype(BF)
-            W_[1, t, rows(r), :] = nn(xT[rows(r), M:L], gp[t]).astype(BF)
+        gi = (nn(low[...], W_[2, t]) * gp[t].astype(F32)).astype(BF)
+        gp[t] = gi
+        SM[pl.ds(2 * T + t, 1), :] += colsum(gi.astype(F32))
+        gz[...] += nt(gi, W_[1, t])
+        W_[2, t] = nn(xT[:, 0:M], hid[t]).astype(BF)
+        W_[1, t] = nn(xT[:, M:L], gi).astype(BF)
 
     sum_start(2)
     sum_start(1)
@@ -536,18 +577,14 @@
 
     @pl.loop(0, T)
     def _(t):
-        @pl.loop(0, M // RB)
-        def _(r):
-            hid[t, rows(r), 0:W] = nn(low[rows(r), :], W_[0, t, :, 3 * W:4 * W]).astype(BF)
-
-        @pl.loop(0, D // RB)
-        def _(r):
-            G0[t, rows(r), 3 * W:4 * W] = nn(xT[rows(r), 0:M], mixed[t, :, 0:W]).astype(BF)
+        hid[t, :, 0:W] = nn(low[...], W_[0, t, :, 3 * W:4 * W]).astype(BF)
+        W_[0, t, :, 3 * W:4 * W] = nn(xT[:, 0:M], mixed[t, :, 0:W]).astype(BF)
 
     @pl.loop(0, T)
     def _(t):
         @pl.when(t == 0)
         def _():
+            hand_on(CO, OF, orcv, 0, 0)
             sum_core(2)
 
         @pl.when(t == 1)
@@ -557,11 +594,11 @@
         @pl.when(t == 2)
         def _():
             sum_turn(2)
-            hand_on(outb, OF, orcv, 0)
 
         @pl.when(t == 3)
         def _():
             sum_turn(1)
+            hand_on(CO, OF, orcv, 0, 1)
 
         vT[...] = k[t, :, 0:W].T
         for pair in range((NH + 1) // 2):
@@ -628,45 +665,40 @@
         SM[...] += srecv[step]
 
     small_start(0)
-    sum_straight(2)
-
     xT[...] = X[...].T
 
     @pl.loop(0, T)
     def _(t):
-        @pl.loop(0, D // RB)
-        def _(r):
-            rr = rows(r)
-            G0[t, rr, 0:W] = nn(xT[rr, pl.ds(pl.multiple_of(own, 128), M)], q[t, :, 0:W]).astype(BF)
-            G0[t, rr, W:2 * W] = nn(xT[rr, :], k[t, :, 0:W]).astype(BF)
-            G0[t, rr, 2 * W:3 * W] = nn(xT[rr, :], v[t, :, 0:W]).astype(BF)
+        W_[0, t, :, 0:W] = nn(xT[:, pl.ds(pl.multiple_of(own, 128), M)], q[t, :, 0:W]).astype(BF)
+        W_[0, t, :, W:2 * W] = nn(xT[...], k[t, :, 0:W]).astype(BF)
+        W_[0, t, :, 2 * W:3 * W] = nn(xT[...], v[t, :, 0:W]).astype(BF)
 
     sum_start(0)
     small_end(0)
     small_start(1)
-    sum_straight(1)
-    sum_core(0)
+    sum_straight(2)
     small_end(1)
     small_start(2)
-    sum_last(2)
-    sum_turn(0)
+    sum_straight(1)
+    hand_on(low, GF, grcv, 4, 0)
+    sum_core(0)
     small_end(2)
     small_start(3)
-    sum_last(1)
+    sum_along(2)
+    sum_turn(0)
     small_end(3)
     small_start(4)
-    hand_on(low, GF, grcv, 2)
+    hand_on(low, GF, grcv, 4, 1)
+    sum_along(1)
     small_end(4)
     sum_straight(0)
-    sum_last(0)
-
-    BQ[...] = SM[pl.ds(z, 1), 0:W]
-    BV[...] = SM[pl.ds(T + z, 1), 0:W]
-    B1[...] = SM[pl.ds(2 * T + z, 1), :]
-    VEC[...] = SM[3 * T:3 * T + 8, :]
-    settle(outb, OF, orcv, 0)
-    settle(low, GF, grcv, 2)
-    pushed(outb, OF, osem, orcv, osl)
+    sum_along(0)
+    for s in (2, 1, 0):
+        sum_last(s)
+    SMO[...] = SM[...]
+    settle(CO, OF, orcv, 0)
+    settle(low, GF, grcv, 4)
+    pushed(CO, OF, osem, orcv, osl)
     pushed(low, GF, gsem, grcv, gsl)
     part.wait_send()
     for step in range(5):
@@ -677,11 +709,11 @@
             straight(s, kk).wait_send()
         turn(s, 0).wait_send()
         turn(s, 1).wait_send()
-        for d in range(1, T):
-            last(s, d).wait_send()
-
-
-def layer_call(wq, wk, wv, wo, w1, w2t, norms, biases, lengths, tokens, cotangent, T):
+        sum_sent(s)
+
+
+def layer_call(weights, vectors, lengths, tokens, cotangent, T):
+    wq, w1 = weights[0], weights[4]
     S, W = wq.shape
     D = tokens.shape[1]
     F = w1.shape[1]
@@ -696,21 +728,21 @@
     V = pltpu.VMEM
     return pl.pallas_call(
         layer_kernel,
-        in_specs=[vm] * 8 + [pl.BlockSpec(memory_space=pltpu.SMEM), any_, any_],
-        out_specs=[any_, any_] + [vm] * 10,
+        in_specs=[vm] * (len(weights) + len(vectors)) + [pl.BlockSpec(memory_space=pltpu.SMEM), any_, any_],
+        out_specs=[any_, any_, vm, vm],
         out_shape=[
             jax.ShapeDtypeStruct((4 * M, D), BF),
             jax.ShapeDtypeStruct((4 * M, D), BF),
-            f32(S, W), f32(S, W), f32(S, W), f32(W, S), f32(S, F), f32(F, S),
-            f32(1, W), f32(1, W), f32(1, F), f32(8, D),
+            f32(SL, S, D), f32(24, D),
         ],
         scratch_shapes=[
             V((SL, S, D), BF),
             V((SL, T, D, F), BF),
-            V((T, D, D), BF),
             V((L, D), BF),
             V((M, D), BF),
             V((2, 8, L), F32),
+            V((8, D), F32),
+            V((8, D), F32),
             V((T, 8, D), F32),
             V((24, D), F32),
             V((T, M, WP), BF),
@@ -730,34 +762,90 @@
             V((M, D), BF),
             V((D, L), BF),
             V((M, D), BF),
-            V((M, D), BF),
             V((SL, 4, T, S, D), BF),
             V((SL, 2, 2, S, D), BF),
             V((SL, 2, T, S, D), BF),
-            V((SL, T - 1, S, D), BF),
+            V((SL, 2, T, S, D), BF),
             V((5, 24, D), F32),
             V((5, 24, D), F32),
             dma((2,)),
-            dma((SL, T - 1)), dma((SL, T - 1)),
+            dma((SL, 2)), dma((SL, T)), dma((SL, T)),
             dma((3, SL, T)), dma((SL, T)), dma((SL, T)), dma((4, SL, T)),
             dma((SL, T)), dma((SL, T)),
             dma((3, SL, T)),
             dma((T - 1,)), dma((T - 1,)),
             dma((3,)), dma((3,)),
             dma, dma,
-            dma((5,)), dma((4,)), dma,
-            dma((5,)), dma((4,)), dma,
-            dma((4,)),
+            dma((3,)), dma((4,)), dma,
+            dma((3,)), dma((4,)), dma,
+            dma((8,)),
             dma((SL, 4)), dma((SL, 4)),
             dma((SL, 2)), dma((SL, 2)),
             dma((SL, 4)), dma((SL, 4)),
-            dma((SL, T - 1)), dma((SL, T - 1)),
+            dma((SL, 2, T)), dma((SL, 2, T)),
             dma((5,)), dma((5,)),
         ],
         compiler_params=pltpu.CompilerParams(
             collective_id=0, has_side_effects=True, vmem_limit_bytes=64 << 20
         ),
-    )(wq, wk, wv, wo, w1, w2t, norms, biases, lengths, tokens, cotangent)
+    )(*weights, *vectors, lengths, tokens, cotangent)
+
+
+def finish_kernel(OF, GF, GR, SMO, OUT, GT, DQ, DK, DV, DO, D1, D2, BQ, BV, B1, BO, G1, S1, B2, G2, S2, keep, gr, sm, came, went, here):
+    z = lax.axis_index("tensor")
+    T = lax.axis_size("tensor")
+    W = DQ.shape[1]
+    n = keep.shape[1]
+    size = keep.shape[2]
+    ins, outs = [], []
+    small = [pltpu.make_async_copy(GR, gr, here.at[0]), pltpu.make_async_copy(SMO, sm, here.at[1])]
+    for a, (src, dst) in enumerate(((GF, GT), (OF, OUT))):
+        for i in range(n):
+            part = pl.ds(i * size, size)
+            ins.append(pltpu.make_async_copy(src.at[part], keep.at[a, i], came.at[a, i]))
+            outs.append(pltpu.make_async_copy(keep.at[a, i], dst.at[part], went.at[a, i]))
+    for copy in small + ins:
+        copy.start()
+    for copy in small:
+        copy.wait()
+    DQ[...] = gr[0, :, 0:W]
+    DK[...] = gr[0, :, W:2 * W]
+    DV[...] = gr[0, :, 2 * W:3 * W]
+    DO[...] = gr[0, :, 3 * W:4 * W].T
+    D1[...] = gr[1]
+    D2[...] = gr[2]
+    BQ[...] = sm[pl.ds(z, 1), 0:W].reshape(W)
+    BV[...] = sm[pl.ds(T + z, 1), 0:W].reshape(W)
+    B1[...] = sm[pl.ds(2 * T + z, 1), :].reshape(B1.shape[0])
+    for i, ref in enumerate((BO, B2, G1, S1, G2, S2)):
+        ref[...] = sm[3 * T + i:3 * T + i + 1, :].reshape(ref.shape[0])
+    for a, b in zip(ins, outs):
+        a.wait()
+        b.start()
+    for copy in outs:
+        copy.wait()
+
+
+def finish_call(full, grads, gr, sm, T):
+    SL, S, D = gr.shape
+    W = D // T
+    n = 8
+    any_ = pl.BlockSpec(memory_space=pltpu.HBM)
+    vm = pl.BlockSpec(memory_space=pltpu.VMEM)
+    f32 = lambda *s: jax.ShapeDtypeStruct(s, F32)
+    same = jax.ShapeDtypeStruct(full.shape, full.dtype)
+    return pl.pallas_call(
+        finish_kernel,
+        in_specs=[any_] * 4,
+        out_specs=[any_, any_] + [vm] * 15,
+        out_shape=[same, same, f32(S, W), f32(S, W), f32(S, W), f32(W, S), f32(S, D), f32(S, D),
+                   f32(W), f32(W), f32(D), f32(D), f32(D), f32(D), f32(D), f32(D), f32(D)],
+        scratch_shapes=[
+            pltpu.VMEM((2, n, full.shape[0] // n, D), BF), pltpu.VMEM(gr.shape, F32), pltpu.VMEM(sm.shape, F32),
+            pltpu.SemaphoreType.DMA((2, n)), pltpu.SemaphoreType.DMA((2, n)), pltpu.SemaphoreType.DMA((2,)),
+        ],
+        compiler_params=pltpu.CompilerParams(vmem_limit_bytes=64 << 20),
+    )(full, grads, gr, sm)
 
 
 def doc_ids(lengths, count):
@@ -1057,16 +1145,11 @@
 
 def split_body(T, tokens, doc_lengths, wq, bq, wk, wv, bv, wo, bo, gain1, shift1, w1, b1, w2, b2,
                gain2, shift2, cotangent):
-    S, W = wq.shape
-    D = tokens.shape[1]
-    F = w1.shape[1]
-    row = lambda x: jnp.pad(x[None, :], ((0, 0), (0, D - x.shape[0])))
-    biases = jnp.concatenate([row(b1), row(bq), row(bv), jnp.zeros((5, D), F32)])
-    norms = jnp.stack([bo, gain1, shift1, b2, gain2, shift2, bo, bo])
-    (full, grads, dq, dk, dv, do, d1, d2, gbq, gbv, gb1, vec) = layer_call(
-        wq, wk, wv, wo, w1, w2.T, norms, biases, doc_lengths, tokens, cotangent, T)
-    return (full, grads, dq, gbq[0], dk, dv, gbv[0], do, vec[0], vec[2], vec[3], d1, gb1[0], d2,
-            vec[1], vec[4], vec[5])
+    weights = (wq, wk, wv, wo, w1, w2.T)
+    vectors = (bo, gain1, shift1, b2, gain2, shift2, b1, bq, bv)
+    (full, grads, dq, dk, dv, do, d1, d2, gbq, gbv, gb1, gbo, gg1, gs1, gb2, gg2, gs2) = finish_call(
+        *layer_call(weights, vectors, doc_lengths, tokens, cotangent, T), T)
+    return full, grads, dq, gbq, dk, dv, gbv, do, gbo, gg1, gs1, d1, gb1, d2.T, gb2, gg2, gs2
 
 
 def solution(mesh):

time: 280 us -> 225 us (0.80)
  Pallas kernels: 257 us -> 224 us
  local copies, waits for them, and re-layouts: 19 us -> 0 us
    pallas_call x1 -> x2, Pallas kernels: 257 us -> 224 us  [the longest x1 217 us: layer_call(): pl.pallas_call(layer_kernel, in_specs=[vm] * (len(weights) + len(vectors)...]
    unnamed x26 -> x0, local copies, waits for them, and re-layouts: 11.9 us -> none
    another operation x7 -> x0, local copies, waits for them, and re-layouts: 4.78 us -> none  [split_body(): norms = jnp.stack([bo, gain1, shift1, b2, gain2, shift2, bo, bo])]
where the time goes in v3:
time: 225 us
  Pallas kernels  224 us (100%)
    pallas_call x1, Pallas kernels, layer_call(): pl.pallas_call(layer_kernel, in_specs=[vm] * (len(weights) + len(vectors)...  217 us
    pallas_call x1, Pallas kernels, finish_call(): pl.pallas_call(finish_kernel, in_specs=[any_] * 4, out_specs=[any_, any_]...  7.16 us

profile of v3, /device:TPU:1, one launch (start us, length us, event | category | flops | bytes accessed | tf_op | source)
XLA Modules:
  0.0 225.1 jit_solution(2766614907280936477)
XLA Ops:
  0.7 217.1 %shard_map.305 = (bf16[2048,768]{1,0:T(8,128)(2,1)}, bf16[2048,768]{1,0:T(8,128)(2,1)}, f32[3,96,768]{2,1,0:T(8,128)}, f32[24,768]{1,0:T(8,128)}) custom-call(bf16[96,192]{1,0:T(8,128)(2,1)} %WQ.1, bf16[96,192]{1,0:T(8,128)(2,1)} %WK.1, bf16[96,192]{1,0:T(8,128)(2,1)} %WV.1, bf16[192,96]{1,0:T(8,128)(2,1)} %WO.1, bf16[96,768]{1,0:T(8,128)(2,1)} %W1.1, ...), custom_call_target="tpu_custom_call" | custom-call | tf_op jit(solution)/shard_map/pallas_call | solution.py:729
  217.8 7.2 %shard_map.306 = (bf16[2048,768]{1,0:T(8,128)(2,1)}, bf16[2048,768]{1,0:T(8,128)(2,1)}, f32[96,192]{1,0:T(8,128)}, f32[96,192]{1,0:T(8,128)}, f32[96,192]{1,0:T(...) custom-call(bf16[2048,768]{1,0:T(8,128)(2,1)} %get-tuple-element.38., ...), custom_call_target="tpu_custom_call" | custom-call | tf_op jit(solution)/shard_map/pallas_call | solution.py:837

commit v4 on v3

--- a/solution.py
+++ b/solution.py
@@ -50,7 +50,7 @@
     PK, W_, X, CO, SG, NP, BP, BI, SM,
     q, k, v, mixed, vT, oT, lse, bias, n1, r1, flow, hid, gp, gz, low, xT,
     rgt, rc, ra, rb, rz, ssend, srecv,
-    loc, zs, zf, zr, os_, xr, yr, cr, fs, dr, ks, bs, br, ts, tr,
+    loc, us, ur, zs, zf, zr, os_, xr, yr, cr, fs, dr, ks, bs, br, ts, tr,
     gs, gr, osem, orcv, osl, gsem, grcv, gsl, fwd, cs, crr, s1, q1, s2, q2, s3, q3, ms, mr,
 ):
     SL, S, D = PK.shape
@@ -110,8 +110,10 @@
         pl.semaphore_signal(barrier, inc=1, device_id=friend, device_id_type=MESH)
     pl.semaphore_wait(barrier, len(friends))
 
-    def block(s, t, i):
-        return W_.at[s, t, pl.ds(pl.multiple_of(i * S, S), S), :]
+    CUT = S // 2
+
+    def late(t, i):
+        return W_.at[SL - 1, t, pl.ds(pl.multiple_of(i * S + CUT, CUT), CUT), :]
 
     half = z // 2
 
@@ -124,96 +126,163 @@
     right, left = (dp, (z + 1) % T), (dp, (z + T - 1) % T)
     can_right, can_left = z < T - 1, z > 0
 
-    def send_z(s):
+    def each(s, copies):
+        if isinstance(s, int):
+            copies(CUT if s == SL - 1 else S)
+        else:
+            pl.when(s < SL - 1)(lambda: copies(S))
+            pl.when(s == SL - 1)(lambda: copies(CUT))
+
+    def shard(s, n):
+        return PK.at[s, 0:n, :]
+
+    def block(s, t, i, n):
+        return W_.at[s, t, pl.ds(pl.multiple_of(i * S, S), n), :]
+
+    def send_z(s, n):
         return (
-            (can_right, remote(PK.at[s], block(s, z, dp), zs.at[s, 0], zr.at[s, z], right)),
-            (can_left, remote(PK.at[s], block(s, z, dp), zs.at[s, 1], zr.at[s, z], left)),
+            (can_right, remote(shard(s, n), block(s, z, dp, n), zs.at[s, 0], zr.at[s, z], right)),
+            (can_left, remote(shard(s, n), block(s, z, dp, n), zs.at[s, 1], zr.at[s, z], left)),
         )
 
-    def pass_z(s, t):
-        here = block(s, t, dp)
+    def pass_z(s, t, n):
+        here = block(s, t, dp, n)
         return (
             (can_right & (t < z), remote(here, here, zf.at[s, t], zr.at[s, t], right)),
             (can_left & (t > z), remote(here, here, zf.at[s, t], zr.at[s, t], left)),
         )
 
     def push_z(s):
-        for able, copy in send_z(s):
+        for able, copy in send_z(s, CUT if s == SL - 1 else S):
             pl.when(able)(copy.start)
 
-    def send_block(s, d, src):
+    def send_block(s, d, src, n):
         t = source(d)
-        remote(src, block(s, t, dp), os_.at[0, s, d], xr.at[s, d], (dpx, z)).start()
-        remote(src, block(s, t, dp), os_.at[1, s, d], yr.at[s, d], (dpy, z)).start()
-        remote(src, block(s, t, dp), os_.at[2, s, d], cr.at[0, s, d], (dpc, z)).start()
-
-    def pass_core(kind, s, d, i):
+        remote(src, block(s, t, dp, n), os_.at[0, s, d], xr.at[s, d], (dpx, z)).start()
+        remote(src, block(s, t, dp, n), os_.at[1, s, d], yr.at[s, d], (dpy, z)).start()
+        remote(src, block(s, t, dp, n), os_.at[2, s, d], cr.at[0, s, d], (dpc, z)).start()
+
+    def pass_core(kind, s, d, i, n):
+        here = block(s, source(d), i, n)
+        remote(here, here, ks.at[kind - 1, s, d], cr.at[kind, s, d], (dpc, z)).start()
+
+    def take_z(s, d, n):
         t = source(d)
-        remote(block(s, t, i), block(s, t, i), ks.at[kind - 1, s, d], cr.at[kind, s, d], (dpc, z)).start()
-
-    def take_z(s, d):
+        remote(shard(s, n), block(s, t, dp, n), zs.at[s, 0], zr.at[s, t], right).wait_recv()
+        for able, copy in pass_z(s, t, n):
+            pl.when(able)(copy.start)
+        send_block(s, d, block(s, t, dp, n), n)
+
+    def take_xy(s, d, n):
         t = source(d)
-        remote(PK.at[s], block(s, t, dp), zs.at[s, 0], zr.at[s, t], right).wait_recv()
-        for able, copy in pass_z(s, t):
-            pl.when(able)(copy.start)
-        send_block(s, d, block(s, t, dp))
-
-    def take_x(s, d):
-        t = source(d)
-        remote(PK.at[s], block(s, t, dpx), os_.at[0, s, d], xr.at[s, d], (dpx, z)).wait_recv()
+        fromx, fromy = block(s, t, dpx, n), block(s, t, dpy, n)
+        remote(shard(s, n), fromx, os_.at[0, s, d], xr.at[s, d], (dpx, z)).wait_recv()
 
         @pl.when(d < T // 2)
         def _():
-            remote(block(s, t, dpx), block(s, t, dpx), fs.at[s, d], dr.at[s, d], (dpy, z)).start()
-
-        pass_core(1, s, d, dpx)
-
-    def take_y(s, d):
-        t = source(d)
-        remote(PK.at[s], block(s, t, dpy), os_.at[1, s, d], yr.at[s, d], (dpy, z)).wait_recv()
+            remote(fromx, fromx, fs.at[s, d], dr.at[s, d], (dpy, z)).start()
+
+        pass_core(1, s, d, dpx, n)
+        remote(shard(s, n), fromy, os_.at[1, s, d], yr.at[s, d], (dpy, z)).wait_recv()
 
         @pl.when(d >= T // 2)
         def _():
-            remote(block(s, t, dpy), block(s, t, dpy), fs.at[s, d], dr.at[s, d], (dpx, z)).start()
-
-        pass_core(2, s, d, dpy)
-
-    def take_diag(s, d):
-        remote(PK.at[s], block(s, source(d), dpxy), fs.at[s, d], dr.at[s, d], (dpx, z)).wait_recv()
-        pass_core(3, s, d, dpxy)
+            remote(fromy, fromy, fs.at[s, d], dr.at[s, d], (dpx, z)).start()
+
+        pass_core(2, s, d, dpy, n)
+
+    def take_diag(s, d, n):
+        remote(shard(s, n), block(s, source(d), dpxy, n), fs.at[s, d], dr.at[s, d], (dpx, z)).wait_recv()
+        pass_core(3, s, d, dpxy, n)
+
+    def late_to(way, i, who):
+        src = PK.at[SL - 1, CUT:S, :] if way < 2 else late(z, i)
+        return remote(src, late(z, i), us.at[way], ur.at[way], who)
+
+    chips = (dp, dpx, dpy, dpxy)
+
+    def bundle(t, send, recv, who):
+        return [remote(late(t, i), late(t, i), us.at[send], ur.at[recv], who) for i in chips]
+
+    def whole(t, send, recv, who):
+        every = W_.at[SL - 1, t, 0:4 * CUT, :]
+        return remote(every, every, us.at[send], ur.at[recv], who)
+
+    def late_core(t):
+        for copy in bundle(t, 5 + T + t, 3 + T + t, (dpc, z)):
+            copy.start()
+
+    def late_start():
+        late_to(0, dp, (dpx, z)).start()
+        late_to(1, dp, (dpy, z)).start()
+
+    def late_turn():
+        late_to(0, dpx, (dpx, z)).wait_recv()
+        late_to(2, dpx, (dpy, z)).start()
+
+    def late_along():
+        late_to(1, dpy, (dpy, z)).wait_recv()
+        late_to(2, dpxy, (dpy, z)).wait_recv()
+        for able, send, who in ((can_right, 3, right), (can_left, 4, left)):
+            @pl.when(able)
+            def _():
+                for copy in bundle(z, send, 3 + z, who):
+                    copy.start()
+        late_core(z)
+
+    def late_pass(t):
+        whole(t, 3, 3 + t, right).wait_recv()
+        for able, who in ((can_right & (t < z), right), (can_left & (t > z), left)):
+            @pl.when(able)
+            def _():
+                for copy in bundle(t, 5 + t, 3 + t, who):
+                    copy.start()
+        late_core(t)
+
+    def late_sent():
+        for way, who in ((0, dpx), (1, dpy), (2, dpy)):
+            late_to(way, dp, (who, z)).wait_send()
+        pl.when(can_right)(whole(z, 3, 3, right).wait_send)
+        pl.when(can_left)(whole(z, 4, 3, left).wait_send)
+        for t in range(T):
+            pl.when((can_right & (t < z)) | (can_left & (t > z)))(whole(t, 5 + t, 3, right).wait_send)
+            whole(t, 5 + T + t, 3, (dpc, z)).wait_send()
 
     PIECES = SL * T
     XL, DL = 2, 4
     STEPS = PIECES + DL
-    first_steps = DL + 1
+    first_steps = DL
 
     def gather_step(n):
         n = jnp.int32(n)
 
-        @pl.when(n < PIECES)
-        def _():
-            s, d = n // T, n % T
-
-            @pl.when(d > 0)
+        def piece(lag, what):
+            @pl.when((n >= lag) & (n < PIECES + lag))
             def _():
-                take_z(s, d)
-
-            @pl.when(d == 0)
-            def _():
-                send_block(s, d, PK.at[s])
-
-        @pl.when((n >= XL) & (n < PIECES + XL))
-        def _():
-            take_x((n - XL) // T, (n - XL) % T)
-            take_y((n - XL) // T, (n - XL) % T)
-
-        @pl.when((n >= DL) & (n < PIECES + DL))
-        def _():
-            take_diag((n - DL) // T, (n - DL) % T)
+                s, d = (n - lag) // T, (n - lag) % T
+                each(s, lambda size: what(s, d, size))
+
+        def arrive(s, d, size):
+            pl.when(d > 0)(lambda: take_z(s, d, size))
+            pl.when(d == 0)(lambda: send_block(s, d, shard(s, size), size))
+
+        piece(0, arrive)
+        for when, act in LATE:
+            pl.when(n == when)(act)
+        piece(XL, take_xy)
+        piece(DL, take_diag)
+
+    LATE = (
+        (0, late_start), (2, late_turn), (4, late_along),
+        (7, lambda: late_pass(source(1))), (9, lambda: late_pass(source(2))), (11, lambda: late_pass(source(3))),
+    )
 
     def gathered(s, d):
+        n = CUT if s == SL - 1 else S
         for kind, i in enumerate((dpc, dpx + flip, dpy + flip, dpxy + flip)):
-            remote(PK.at[s], block(s, source(d), i), os_.at[2, s, d], cr.at[kind, s, d], (dpc, z)).wait_recv()
+            remote(shard(s, n), block(s, source(d), i, n), os_.at[2, s, d], cr.at[kind, s, d], (dpc, z)).wait_recv()
+        if s == SL - 1:
+            whole(source(d), 3, 3 + T + source(d), (dpc, z)).wait_recv()
 
     for s in range(SL):
         push_z(s)
@@ -299,21 +368,19 @@
 
     @pl.loop(0, T)
     def _(t):
+        vT[...] = v[t, :, 0:W].T
+
+        for j in range(NH):
+            s = nt(head(k, t, everything, j), only(head(q, t, everything, j), j)) + bias[...]
+            m = jnp.max(s, axis=0, keepdims=True)
+            p = jnp.exp(s - m)
+            l = jnp.sum(p, axis=0, keepdims=True)
+            lse[t * 4 + j] = jnp.broadcast_to(m + jnp.log(l), (8, M))
+            o = nn(vT[j * HD:(j + 1) * HD, :], p.astype(BF))
+            oT[j * HD:(j + 1) * HD, :] = o * (1.0 / l)
+
+        mixed[t, :, 0:W] = oT[...].T.astype(BF)
         gather_step(first_steps + T + t)
-        vT[...] = v[t, :, 0:W].T
-
-        for i in range(M // QC):
-            qs = slice(i * QC, (i + 1) * QC)
-            for j in range(NH):
-                s = nt(head(k, t, everything, j), only(head(q, t, qs, j), j)) + bias[:, qs]
-                m = jnp.max(s, axis=0, keepdims=True)
-                p = jnp.exp(s - m)
-                l = jnp.sum(p, axis=0, keepdims=True)
-                lse[t * 4 + j, :, qs] = jnp.broadcast_to(m + jnp.log(l), (8, QC))
-                o = nn(vT[j * HD:(j + 1) * HD, :], p.astype(BF))
-                oT[j * HD:(j + 1) * HD, qs] = o * (1.0 / l)
-
-        mixed[t, :, 0:W] = oT[...].T.astype(BF)
 
     @pl.loop(0, M // RB)
     def _(r):
@@ -364,33 +431,37 @@
 
     dest = dp - core + home
 
-    def spotrows(zz, cc):
-        return pl.ds(pl.multiple_of(((zz % 2) * 2 + cc) * M, M), M)
+    PARTS = 2
+    PR = M // PARTS
+
+    def spotrows(b, cc, part):
+        return pl.ds(pl.multiple_of(((b % 2) * 2 + cc) * M + part * PR, PR), PR)
+
+    def spotsem(b, cc, part):
+        return ((b % 2) * 2 + cc) * PARTS + part
 
     def pushes(src, full, sems, recv):
         return [
-            (able, remote(src, full.at[spotrows(z, core)], sems.at[i], recv.at[(z % 2) * 2 + core], (dest, chip)))
-            for i, (able, chip) in enumerate(((can_right, (z + 1) % T), (can_left, (z + T - 1) % T)))
+            (able, remote(src.at[pl.ds(part * PR, PR)], full.at[spotrows(z, core, part)],
+                          sems.at[i * PARTS + part], recv.at[spotsem(z, core, part)], chip))
+            for part in range(PARTS)
+            for i, (able, chip) in enumerate((
+                (can_right, (dest, (z + 1) % T)), (can_left, (dest, (z + T - 1) % T)), (core != home, (dpc, z))))
         ]
 
-    def own_copy(src, full, sems, recv, slot):
-        away = remote(src, full.at[spotrows(z, core)], sems.at[2], recv.at[(z % 2) * 2 + core], (dpc, z))
-        here = pltpu.make_async_copy(src, full.at[spotrows(z, core)], slot)
-        return away, here
+    def here(src, full, slot):
+        rows_ = pl.ds(pl.multiple_of(((z % 2) * 2 + core) * M, M), M)
+        return pltpu.make_async_copy(src, full.at[rows_], slot)
 
     def push(src, full, sems, recv, slot):
         for able, copy in pushes(src, full, sems, recv):
             pl.when(able)(copy.start)
-        away, here = own_copy(src, full, sems, recv, slot)
-        pl.when(core != home)(away.start)
-        pl.when(core == home)(here.start)
+        pl.when(core == home)(here(src, full, slot).start)
 
     def pushed(src, full, sems, recv, slot):
         for able, copy in pushes(src, full, sems, recv):
             pl.when(able)(copy.wait_send)
-        away, here = own_copy(src, full, sems, recv, slot)
-        pl.when(core != home)(away.wait_send)
-        pl.when(core == home)(here.wait)
+        pl.when(core == home)(here(src, full, slot).wait)
 
     ahead = 1 - 2 * core
 
@@ -399,20 +470,21 @@
             return (z == 1) | (z == 2)
         return z == 2 - core
 
-    def got(src, full, recv, b, cc):
-        remote(src, full.at[spotrows(b, cc)], gs, recv.at[(b % 2) * 2 + cc], (dpx, z)).wait_recv()
-
-    def handing(full, recv, base, hop, cc):
+    def got(src, full, recv, b, cc, part):
+        remote(src.at[0:PR], full.at[spotrows(b, cc, part)], gs, recv.at[spotsem(b, cc, part)], (dpx, z)).wait_recv()
+
+    def handing(full, recv, base, hop, cc, part):
         b = z - ahead * (hop + 1)
-        return remote(full.at[spotrows(b, cc)], full.at[spotrows(b, cc)], fwd.at[base + 2 * hop + cc],
-                      recv.at[(b % 2) * 2 + cc], (dp, (z + ahead) % T))
-
-    def hand_on(src, full, recv, base, hop):
+        spot_ = full.at[spotrows(b, cc, part)]
+        return remote(spot_, spot_, fwd.at[base + (2 * hop + cc) * PARTS + part],
+                      recv.at[spotsem(b, cc, part)], (dp, (z + ahead) % T))
+
+    def hand_on(src, full, recv, base, hop, part):
         @pl.when(moves(hop))
         def _():
             for cc in range(2):
-                got(src, full, recv, z - ahead * (hop + 1), cc)
-                handing(full, recv, base, hop, cc).start()
+                got(src, full, recv, z - ahead * (hop + 1), cc, part)
+                handing(full, recv, base, hop, cc, part).start()
 
     def settle(src, full, recv, base):
         for kk in range(2):
@@ -422,27 +494,31 @@
 
                 @pl.when(jnp.logical_not((b == z) & (core == cc)) & jnp.logical_not(gone))
                 def _():
-                    got(src, full, recv, b, cc)
+                    for part in range(PARTS):
+                        got(src, full, recv, b, cc, part)
 
         for hop in range(2):
             @pl.when(moves(hop))
             def _():
                 for cc in range(2):
-                    handing(full, recv, base, hop, cc).wait_send()
+                    for part in range(PARTS):
+                        handing(full, recv, base, hop, cc, part).wait_send()
 
     push(CO, OF, osem, orcv, osl)
 
     for s in range(SL):
-        for able, copy in send_z(s):
+        n = CUT if s == SL - 1 else S
+        for able, copy in send_z(s, n):
             pl.when(able)(copy.wait_send)
         for t in range(T):
-            for able, copy in pass_z(s, t):
+            for able, copy in pass_z(s, t, n):
                 pl.when(able)(copy.wait_send)
         for d in range(T):
             for kind in range(3):
-                remote(PK.at[s], block(s, z, dp), os_.at[kind, s, d], xr.at[s, d], (dpx, z)).wait_send()
-                remote(PK.at[s], block(s, z, dp), ks.at[kind, s, d], xr.at[s, d], (dpx, z)).wait_send()
-            remote(PK.at[s], block(s, z, dp), fs.at[s, d], xr.at[s, d], (dpx, z)).wait_send()
+                remote(shard(s, n), block(s, z, dp, n), os_.at[kind, s, d], xr.at[s, d], (dpx, z)).wait_send()
+                remote(shard(s, n), block(s, z, dp, n), ks.at[kind, s, d], xr.at[s, d], (dpx, z)).wait_send()
+            remote(shard(s, n), block(s, z, dp, n), fs.at[s, d], xr.at[s, d], (dpx, z)).wait_send()
+    late_sent()
     for d in range(1, T):
         remote(BP, BI.at[z], bs.at[d - 1], br.at[d - 1], (dp, (z + d) % T)).wait_send()
 
@@ -557,6 +633,7 @@
         W_[2, t] = nn(xT[:, 0:M], hid[t]).astype(BF)
         W_[1, t] = nn(xT[:, M:L], gi).astype(BF)
 
+    hand_on(CO, OF, orcv, 0, 0, 0)
     sum_start(2)
     sum_start(1)
 
@@ -578,13 +655,12 @@
     @pl.loop(0, T)
     def _(t):
         hid[t, :, 0:W] = nn(low[...], W_[0, t, :, 3 * W:4 * W]).astype(BF)
-        W_[0, t, :, 3 * W:4 * W] = nn(xT[:, 0:M], mixed[t, :, 0:W]).astype(BF)
 
     @pl.loop(0, T)
     def _(t):
         @pl.when(t == 0)
         def _():
-            hand_on(CO, OF, orcv, 0, 0)
+            hand_on(CO, OF, orcv, 0, 0, 1)
             sum_core(2)
 
         @pl.when(t == 1)
@@ -594,11 +670,12 @@
         @pl.when(t == 2)
         def _():
             sum_turn(2)
+            hand_on(CO, OF, orcv, 0, 1, 0)
 
         @pl.when(t == 3)
         def _():
             sum_turn(1)
-            hand_on(CO, OF, orcv, 0, 1)
+            hand_on(CO, OF, orcv, 0, 1, 1)
 
         vT[...] = k[t, :, 0:W].T
         for pair in range((NH + 1) // 2):
@@ -665,6 +742,11 @@
         SM[...] += srecv[step]
 
     small_start(0)
+
+    @pl.loop(0, T)
+    def _(t):
+        W_[0, t, :, 3 * W:4 * W] = nn(xT[:, 0:M], mixed[t, :, 0:W]).astype(BF)
+
     xT[...] = X[...].T
 
     @pl.loop(0, T)
@@ -674,30 +756,32 @@
         W_[0, t, :, 2 * W:3 * W] = nn(xT[...], v[t, :, 0:W]).astype(BF)
 
     sum_start(0)
+    hand_on(low, GF, grcv, 8, 0, 0)
     small_end(0)
     small_start(1)
-    sum_straight(2)
+    sum_core(0)
+    hand_on(low, GF, grcv, 8, 0, 1)
     small_end(1)
     small_start(2)
-    sum_straight(1)
-    hand_on(low, GF, grcv, 4, 0)
-    sum_core(0)
+    sum_straight(2)
+    sum_turn(0)
+    hand_on(low, GF, grcv, 8, 1, 0)
+    sum_along(2)
     small_end(2)
     small_start(3)
-    sum_along(2)
-    sum_turn(0)
+    sum_straight(1)
+    hand_on(low, GF, grcv, 8, 1, 1)
+    sum_along(1)
     small_end(3)
     small_start(4)
-    hand_on(low, GF, grcv, 4, 1)
-    sum_along(1)
-    small_end(4)
     sum_straight(0)
     sum_along(0)
+    small_end(4)
     for s in (2, 1, 0):
         sum_last(s)
     SMO[...] = SM[...]
     settle(CO, OF, orcv, 0)
-    settle(low, GF, grcv, 4)
+    settle(low, GF, grcv, 8)
     pushed(CO, OF, osem, orcv, osl)
     pushed(low, GF, gsem, grcv, gsl)
     part.wait_send()
@@ -769,6 +853,7 @@
             V((5, 24, D), F32),
             V((5, 24, D), F32),
             dma((2,)),
+            dma((5 + 2 * T,)), dma((3 + 2 * T,)),
             dma((SL, 2)), dma((SL, T)), dma((SL, T)),
             dma((3, SL, T)), dma((SL, T)), dma((SL, T)), dma((4, SL, T)),
             dma((SL, T)), dma((SL, T)),
@@ -776,9 +861,9 @@
             dma((T - 1,)), dma((T - 1,)),
             dma((3,)), dma((3,)),
             dma, dma,
-            dma((3,)), dma((4,)), dma,
-            dma((3,)), dma((4,)), dma,
-            dma((8,)),
+            dma((6,)), dma((8,)), dma,
+            dma((6,)), dma((8,)), dma,
+            dma((16,)),
             dma((SL, 4)), dma((SL, 4)),
             dma((SL, 2)), dma((SL, 2)),
             dma((SL, 4)), dma((SL, 4)),
@@ -791,58 +876,62 @@
     )(*weights, *vectors, lengths, tokens, cotangent)
 
 
-def finish_kernel(OF, GF, GR, SMO, OUT, GT, DQ, DK, DV, DO, D1, D2, BQ, BV, B1, BO, G1, S1, B2, G2, S2, keep, gr, sm, came, went, here):
+def finish_kernel(OF, GF, GR, SMO, OUT, GT, *rest):
+    outs, (keep, gr, sm, *bufs, came, went, read, wrote) = rest[:15], rest[15:]
     z = lax.axis_index("tensor")
     T = lax.axis_size("tensor")
-    W = DQ.shape[1]
-    n = keep.shape[1]
-    size = keep.shape[2]
-    ins, outs = [], []
-    small = [pltpu.make_async_copy(GR, gr, here.at[0]), pltpu.make_async_copy(SMO, sm, here.at[1])]
+    W = bufs[0].shape[1]
+    small = [pltpu.make_async_copy(GR, gr, read.at[0]), pltpu.make_async_copy(SMO, sm, read.at[1])]
+    n, size = keep.shape[1:3]
+    ins, backs = [], []
     for a, (src, dst) in enumerate(((GF, GT), (OF, OUT))):
         for i in range(n):
             part = pl.ds(i * size, size)
             ins.append(pltpu.make_async_copy(src.at[part], keep.at[a, i], came.at[a, i]))
-            outs.append(pltpu.make_async_copy(keep.at[a, i], dst.at[part], went.at[a, i]))
+            backs.append(pltpu.make_async_copy(keep.at[a, i], dst.at[part], went.at[a, i]))
     for copy in small + ins:
         copy.start()
     for copy in small:
         copy.wait()
-    DQ[...] = gr[0, :, 0:W]
-    DK[...] = gr[0, :, W:2 * W]
-    DV[...] = gr[0, :, 2 * W:3 * W]
-    DO[...] = gr[0, :, 3 * W:4 * W].T
-    D1[...] = gr[1]
-    D2[...] = gr[2]
-    BQ[...] = sm[pl.ds(z, 1), 0:W].reshape(W)
-    BV[...] = sm[pl.ds(T + z, 1), 0:W].reshape(W)
-    B1[...] = sm[pl.ds(2 * T + z, 1), :].reshape(B1.shape[0])
-    for i, ref in enumerate((BO, B2, G1, S1, G2, S2)):
+    dq, dk, dv, do, bq, bv, b1 = bufs[:7]
+    dq[...] = gr[0, :, 0:W]
+    dk[...] = gr[0, :, W:2 * W]
+    dv[...] = gr[0, :, 2 * W:3 * W]
+    do[...] = gr[0, :, 3 * W:4 * W].T
+    bq[...] = sm[pl.ds(z, 1), 0:W].reshape(W)
+    bv[...] = sm[pl.ds(T + z, 1), 0:W].reshape(W)
+    b1[...] = sm[pl.ds(2 * T + z, 1), :].reshape(b1.shape[0])
+    for i, ref in zip((0, 2, 3, 1, 4, 5), bufs[7:]):
         ref[...] = sm[3 * T + i:3 * T + i + 1, :].reshape(ref.shape[0])
-    for a, b in zip(ins, outs):
+    sources = [dq, dk, dv, do, gr.at[1], gr.at[2], *bufs[4:]]
+    writes = [pltpu.make_async_copy(src, dst, wrote.at[i]) for i, (src, dst) in enumerate(zip(sources, outs))]
+    for copy in writes:
+        copy.start()
+    for a, b in zip(ins, backs):
         a.wait()
         b.start()
-    for copy in outs:
+    for copy in backs + writes:
         copy.wait()
 
 
 def finish_call(full, grads, gr, sm, T):
     SL, S, D = gr.shape
     W = D // T
-    n = 8
+    n = 4
     any_ = pl.BlockSpec(memory_space=pltpu.HBM)
-    vm = pl.BlockSpec(memory_space=pltpu.VMEM)
     f32 = lambda *s: jax.ShapeDtypeStruct(s, F32)
     same = jax.ShapeDtypeStruct(full.shape, full.dtype)
+    made = [(S, W), (S, W), (S, W), (W, S), (W,), (W,), (D,), (D,), (D,), (D,), (D,), (D,), (D,)]
+    dma = pltpu.SemaphoreType.DMA
     return pl.pallas_call(
         finish_kernel,
         in_specs=[any_] * 4,
-        out_specs=[any_, any_] + [vm] * 15,
-        out_shape=[same, same, f32(S, W), f32(S, W), f32(S, W), f32(W, S), f32(S, D), f32(S, D),
-                   f32(W), f32(W), f32(D), f32(D), f32(D), f32(D), f32(D), f32(D), f32(D)],
+        out_specs=[any_] * 17,
+        out_shape=[same, same] + [f32(*m) for m in made[:4]] + [f32(S, D), f32(S, D)] + [f32(*m) for m in made[4:]],
         scratch_shapes=[
             pltpu.VMEM((2, n, full.shape[0] // n, D), BF), pltpu.VMEM(gr.shape, F32), pltpu.VMEM(sm.shape, F32),
-            pltpu.SemaphoreType.DMA((2, n)), pltpu.SemaphoreType.DMA((2, n)), pltpu.SemaphoreType.DMA((2,)),
+            *[pltpu.VMEM(m, F32) for m in made],
+            dma((2, n)), dma((2, n)), dma((2,)), dma((15,)),
         ],
         compiler_params=pltpu.CompilerParams(vmem_limit_bytes=64 << 20),
     )(full, grads, gr, sm)

time: 225 us -> 207 us (0.920)
  Pallas kernels: 224 us -> 206 us
    pallas_call x1, Pallas kernels: 217 us -> 200 us  [layer_call(): pl.pallas_call(layer_kernel, in_specs=[vm] * (len(weights) + len(vectors)...]
where the time goes in v4:
time: 207 us
  Pallas kernels  206 us (100%)
    pallas_call x1, Pallas kernels, layer_call(): pl.pallas_call(layer_kernel, in_specs=[vm] * (len(weights) + len(vectors)...  200 us
    pallas_call x1, Pallas kernels, finish_call(): pl.pallas_call(finish_kernel, in_specs=[any_] * 4, out_specs=[any_] * 17,...  6.2 us

profile of v4, /device:TPU:1, one launch (start us, length us, event | category | flops | bytes accessed | tf_op | source)
XLA Modules:
  0.0 207.1 jit_solution(5043146253440988115)
XLA Ops:
  0.7 200.1 %shard_map.305 = (bf16[2048,768]{1,0:T(8,128)(2,1)}, bf16[2048,768]{1,0:T(8,128)(2,1)}, f32[3,96,768]{2,1,0:T(8,128)}, f32[24,768]{1,0:T(8,128)}) custom-call(bf16[96,192]{1,0:T(8,128)(2,1)} %WQ.1, bf16[96,192]{1,0:T(8,128)(2,1)} %WK.1, bf16[96,192]{1,0:T(8,128)(2,1)} %WV.1, bf16[192,96]{1,0:T(8,128)(2,1)} %WO.1, bf16[96,768]{1,0:T(8,128)(2,1)} %W1.1, ...), custom_call_target="tpu_custom_call" | custom-call | tf_op jit(solution)/shard_map/pallas_call | solution.py:813
  200.7 6.2 %shard_map.306 = (bf16[2048,768]{1,0:T(8,128)(2,1)}, bf16[2048,768]{1,0:T(8,128)(2,1)}, f32[96,192]{1,0:T(8,128)}, f32[96,192]{1,0:T(8,128)}, f32[96,192]{1,0:T(...) custom-call(bf16[2048,768]{1,0:T(8,128)(2,1)} %get-tuple-element.38., ...), custom_call_target="tpu_custom_call" | custom-call | tf_op jit(solution)/shard_map/pallas_call | solution.py:926

commit v5 on v4

--- a/solution.py
+++ b/solution.py
@@ -60,7 +60,7 @@
     W = D // T
     NH = W // HD
     scale = HD ** (-0.5)
-    QC = RB
+    QC = M
 
     dp = lax.axis_index("dp")
     z = lax.axis_index("tensor")
@@ -158,13 +158,13 @@
 
     def send_block(s, d, src, n):
         t = source(d)
-        remote(src, block(s, t, dp, n), os_.at[0, s, d], xr.at[s, d], (dpx, z)).start()
-        remote(src, block(s, t, dp, n), os_.at[1, s, d], yr.at[s, d], (dpy, z)).start()
-        remote(src, block(s, t, dp, n), os_.at[2, s, d], cr.at[0, s, d], (dpc, z)).start()
+        remote(src, block(s, t, dp, n), os_.at[0, s], xr.at[s, d], (dpx, z)).start()
+        remote(src, block(s, t, dp, n), os_.at[1, s], yr.at[s, d], (dpy, z)).start()
+        remote(src, block(s, t, dp, n), os_.at[2, s], cr.at[s, d], (dpc, z)).start()
 
     def pass_core(kind, s, d, i, n):
         here = block(s, source(d), i, n)
-        remote(here, here, ks.at[kind - 1, s, d], cr.at[kind, s, d], (dpc, z)).start()
+        remote(here, here, ks.at[kind - 1, s], cr.at[s, d], (dpc, z)).start()
 
     def take_z(s, d, n):
         t = source(d)
@@ -176,23 +176,23 @@
     def take_xy(s, d, n):
         t = source(d)
         fromx, fromy = block(s, t, dpx, n), block(s, t, dpy, n)
-        remote(shard(s, n), fromx, os_.at[0, s, d], xr.at[s, d], (dpx, z)).wait_recv()
+        remote(shard(s, n), fromx, os_.at[0, s], xr.at[s, d], (dpx, z)).wait_recv()
 
         @pl.when(d < T // 2)
         def _():
-            remote(fromx, fromx, fs.at[s, d], dr.at[s, d], (dpy, z)).start()
+            remote(fromx, fromx, fs.at[s], dr.at[s, d], (dpy, z)).start()
 
         pass_core(1, s, d, dpx, n)
-        remote(shard(s, n), fromy, os_.at[1, s, d], yr.at[s, d], (dpy, z)).wait_recv()
+        remote(shard(s, n), fromy, os_.at[1, s], yr.at[s, d], (dpy, z)).wait_recv()
 
         @pl.when(d >= T // 2)
         def _():
-            remote(fromy, fromy, fs.at[s, d], dr.at[s, d], (dpx, z)).start()
+            remote(fromy, fromy, fs.at[s], dr.at[s, d], (dpx, z)).start()
 
         pass_core(2, s, d, dpy, n)
 
     def take_diag(s, d, n):
-        remote(shard(s, n), block(s, source(d), dpxy, n), fs.at[s, d], dr.at[s, d], (dpx, z)).wait_recv()
+        remote(shard(s, n), block(s, source(d), dpxy, n), fs.at[s], dr.at[s, d], (dpx, z)).wait_recv()
         pass_core(3, s, d, dpxy, n)
 
     def late_to(way, i, who):
@@ -273,14 +273,14 @@
         piece(DL, take_diag)
 
     LATE = (
-        (0, late_start), (2, late_turn), (4, late_along),
-        (7, lambda: late_pass(source(1))), (9, lambda: late_pass(source(2))), (11, lambda: late_pass(source(3))),
+        (0, late_start), (1, late_turn), (3, late_along),
+        (6, lambda: late_pass(source(1))), (8, lambda: late_pass(source(2))), (10, lambda: late_pass(source(3))),
     )
 
     def gathered(s, d):
         n = CUT if s == SL - 1 else S
-        for kind, i in enumerate((dpc, dpx + flip, dpy + flip, dpxy + flip)):
-            remote(shard(s, n), block(s, source(d), i, n), os_.at[2, s, d], cr.at[kind, s, d], (dpc, z)).wait_recv()
+        four = W_.at[s, source(d), 0:4 * n, :]
+        remote(four, four, os_.at[2, s], cr.at[s, d], (dpc, z)).wait_recv()
         if s == SL - 1:
             whole(source(d), 3, 3 + T + source(d), (dpc, z)).wait_recv()
 
@@ -513,11 +513,11 @@
         for t in range(T):
             for able, copy in pass_z(s, t, n):
                 pl.when(able)(copy.wait_send)
-        for d in range(T):
-            for kind in range(3):
-                remote(shard(s, n), block(s, z, dp, n), os_.at[kind, s, d], xr.at[s, d], (dpx, z)).wait_send()
-                remote(shard(s, n), block(s, z, dp, n), ks.at[kind, s, d], xr.at[s, d], (dpx, z)).wait_send()
-            remote(shard(s, n), block(s, z, dp, n), fs.at[s, d], xr.at[s, d], (dpx, z)).wait_send()
+        four = W_.at[s, z, 0:4 * n, :]
+        for kind in range(3):
+            remote(four, four, os_.at[kind, s], xr.at[s, 0], (dpx, z)).wait_send()
+            remote(four, four, ks.at[kind, s], xr.at[s, 0], (dpx, z)).wait_send()
+        remote(four, four, fs.at[s], xr.at[s, 0], (dpx, z)).wait_send()
     late_sent()
     for d in range(1, T):
         remote(BP, BI.at[z], bs.at[d - 1], br.at[d - 1], (dp, (z + d) % T)).wait_send()
@@ -531,7 +531,7 @@
         return pl.ds(pl.multiple_of(i * S, S), S)
 
     def core_copy(s, kk):
-        return remote(grad(s).at[:, rowsof(rel[kk] + flip), :], rc.at[s, kk], cs.at[s, kk], crr.at[s, kk], (dpc, z))
+        return remote(grad(s).at[:, rowsof(rel[kk] + flip), :], rc.at[s, kk], cs.at[s], crr.at[s, kk], (dpc, z))
 
     def turn(s, kk):
         src, dst, who = (
@@ -660,8 +660,8 @@
     def _(t):
         @pl.when(t == 0)
         def _():
+            sum_core(2)
             hand_on(CO, OF, orcv, 0, 0, 1)
-            sum_core(2)
 
         @pl.when(t == 1)
         def _():
@@ -789,8 +789,8 @@
         small(step).wait_send()
     for s in range(SL):
         for kk in range(4):
-            core_copy(s, kk).wait_send()
             straight(s, kk).wait_send()
+        remote(rc.at[s], rc.at[s], cs.at[s], crr.at[s, 0], (dpc, z)).wait_send()
         turn(s, 0).wait_send()
         turn(s, 1).wait_send()
         sum_sent(s)
@@ -855,16 +855,16 @@
             dma((2,)),
             dma((5 + 2 * T,)), dma((3 + 2 * T,)),
             dma((SL, 2)), dma((SL, T)), dma((SL, T)),
-            dma((3, SL, T)), dma((SL, T)), dma((SL, T)), dma((4, SL, T)),
-            dma((SL, T)), dma((SL, T)),
-            dma((3, SL, T)),
+            dma((3, SL)), dma((SL, T)), dma((SL, T)), dma((SL, T)),
+            dma((SL,)), dma((SL, T)),
+            dma((3, SL)),
             dma((T - 1,)), dma((T - 1,)),
             dma((3,)), dma((3,)),
             dma, dma,
             dma((6,)), dma((8,)), dma,
             dma((6,)), dma((8,)), dma,
             dma((16,)),
-            dma((SL, 4)), dma((SL, 4)),
+            dma((SL,)), dma((SL, 4)),
             dma((SL, 2)), dma((SL, 2)),
             dma((SL, 4)), dma((SL, 4)),
             dma((SL, 2, T)), dma((SL, 2, T)),

time: 207 us -> 202 us (0.976)
  Pallas kernels: 206 us -> 201 us
    pallas_call x1, Pallas kernels: 200 us -> 195 us  [layer_call(): pl.pallas_call(layer_kernel, in_specs=[vm] * (len(weights) + len(vectors)...]
where the time goes in v5:
time: 202 us
  Pallas kernels  201 us (100%)
    pallas_call x1, Pallas kernels, layer_call(): pl.pallas_call(layer_kernel, in_specs=[vm] * (len(weights) + len(vectors)...  195 us
    pallas_call x1, Pallas kernels, finish_call(): pl.pallas_call(finish_kernel, in_specs=[any_] * 4, out_specs=[any_] * 17,...  6.2 us

profile of v5, /device:TPU:1, one launch (start us, length us, event | category | flops | bytes accessed | tf_op | source)
XLA Modules:
  0.0 201.9 jit_solution(15819803496518187993)
XLA Ops:
  0.7 194.9 %shard_map.305 = (bf16[2048,768]{1,0:T(8,128)(2,1)}, bf16[2048,768]{1,0:T(8,128)(2,1)}, f32[3,96,768]{2,1,0:T(8,128)}, f32[24,768]{1,0:T(8,128)}) custom-call(bf16[96,192]{1,0:T(8,128)(2,1)} %WQ.1, bf16[96,192]{1,0:T(8,128)(2,1)} %WK.1, bf16[96,192]{1,0:T(8,128)(2,1)} %WV.1, bf16[192,96]{1,0:T(8,128)(2,1)} %WO.1, bf16[96,768]{1,0:T(8,128)(2,1)} %W1.1, ...), custom_call_target="tpu_custom_call" | custom-call | tf_op jit(solution)/shard_map/pallas_call | solution.py:813
  195.6 6.2 %shard_map.306 = (bf16[2048,768]{1,0:T(8,128)(2,1)}, bf16[2048,768]{1,0:T(8,128)(2,1)}, f32[96,192]{1,0:T(8,128)}, f32[96,192]{1,0:T(8,128)}, f32[96,192]{1,0:T(...) custom-call(bf16[2048,768]{1,0:T(8,128)(2,1)} %get-tuple-element.38., ...), custom_call_target="tpu_custom_call" | custom-call | tf_op jit(solution)/shard_map/pallas_call | solution.py:926

commit v6 on v5

--- a/solution.py
+++ b/solution.py
@@ -440,11 +440,11 @@
     def spotsem(b, cc, part):
         return ((b % 2) * 2 + cc) * PARTS + part
 
-    def pushes(src, full, sems, recv):
+    def pushes(src, full, sems, recv, parts=range(2)):
         return [
             (able, remote(src.at[pl.ds(part * PR, PR)], full.at[spotrows(z, core, part)],
                           sems.at[i * PARTS + part], recv.at[spotsem(z, core, part)], chip))
-            for part in range(PARTS)
+            for part in parts
             for i, (able, chip) in enumerate((
                 (can_right, (dest, (z + 1) % T)), (can_left, (dest, (z + T - 1) % T)), (core != home, (dpc, z))))
         ]
@@ -471,7 +471,7 @@
         return z == 2 - core
 
     def got(src, full, recv, b, cc, part):
-        remote(src.at[0:PR], full.at[spotrows(b, cc, part)], gs, recv.at[spotsem(b, cc, part)], (dpx, z)).wait_recv()
+        remote(src.at[0:PR], full.at[spotrows(b, cc, part)], gs.at[0], recv.at[spotsem(b, cc, part)], (dpx, z)).wait_recv()
 
     def handing(full, recv, base, hop, cc, part):
         b = z - ahead * (hop + 1)
@@ -704,6 +704,9 @@
         SM[pl.ds(t, 1), 0:W] += colsum(dq.astype(F32))
         SM[pl.ds(T + t, 1), 0:W] += colsum(v[t, :, 0:W].astype(F32))
 
+    def share(r):
+        return remote(flow.at[rows(r)], rgt.at[rows(r)], gs.at[r], gr.at[r], (dpc, z))
+
     @pl.loop(0, M // RB)
     def _(r):
         acc = jnp.zeros((RB, D), F32)
@@ -711,9 +714,8 @@
             acc = acc + nt(k[t, othrows(r), 0:W], W_[0, t, :, W:2 * W])
             acc = acc + nt(v[t, othrows(r), 0:W], W_[0, t, :, 2 * W:3 * W])
         flow[rows(r), :] = acc.astype(BF)
-
-    part = remote(flow, rgt, gs, gr, (dpc, z))
-    part.start()
+        share(r).start()
+
 
     @pl.loop(0, M // RB)
     def _(r):
@@ -722,11 +724,15 @@
             acc = acc + nt(q[t, rows(r), 0:W], W_[0, t, :, 0:W])
             acc = acc + nt(k[t, ownrows(r), 0:W], W_[0, t, :, W:2 * W])
             acc = acc + nt(v[t, ownrows(r), 0:W], W_[0, t, :, 2 * W:3 * W])
-        gz[rows(r), :] = acc
-
-    part.wait_recv()
-    low[...] = (gz[...] + rgt[...].astype(F32)).astype(BF)
-    push(low, GF, gsem, grcv, gsl)
+        share(r).wait_recv()
+        low[rows(r), :] = (acc + rgt[rows(r), :].astype(F32)).astype(BF)
+        for part in range(PARTS):
+            @pl.when(r == part)
+            def _():
+                for able, copy in pushes(low, GF, gsem, grcv, (part,)):
+                    pl.when(able)(copy.start)
+
+    pl.when(core == home)(here(low, GF, gsl).start)
 
     pals = [(dpc, z), (dpx, z), (dpy, z), (dp, z + 1 - 2 * (z % 2)), (dp, (z + 2) % T)]
 
@@ -784,7 +790,8 @@
     settle(low, GF, grcv, 8)
     pushed(CO, OF, osem, orcv, osl)
     pushed(low, GF, gsem, grcv, gsl)
-    part.wait_send()
+    share(0).wait_send()
+    share(1).wait_send()
     for step in range(5):
         small(step).wait_send()
     for s in range(SL):
@@ -860,7 +867,7 @@
             dma((3, SL)),
             dma((T - 1,)), dma((T - 1,)),
             dma((3,)), dma((3,)),
-            dma, dma,
+            dma((2,)), dma((2,)),
             dma((6,)), dma((8,)), dma,
             dma((6,)), dma((8,)), dma,
             dma((16,)),

time: 202 us -> 201 us (level)
    pallas_call x1, Pallas kernels: 195 us -> 193 us  [layer_call(): pl.pallas_call(layer_kernel, in_specs=[vm] * (len(weights) + len(vectors)...]
where the time goes in v6:
time: 201 us; the launch traced here: 200 us
  Pallas kernels  199 us (99%)
    pallas_call x1, Pallas kernels, layer_call(): pl.pallas_call(layer_kernel, in_specs=[vm] * (len(weights) + len(vectors)...  193 us
    pallas_call x1, Pallas kernels, finish_call(): pl.pallas_call(finish_kernel, in_specs=[any_] * 4, out_specs=[any_] * 17,...  6.2 us

profile of v6, /device:TPU:1, one launch (start us, length us, event | category | flops | bytes accessed | tf_op | source)
XLA Modules:
  0.0 199.9 jit_solution(10673854046360331727)
XLA Ops:
  0.7 192.8 %shard_map.305 = (bf16[2048,768]{1,0:T(8,128)(2,1)}, bf16[2048,768]{1,0:T(8,128)(2,1)}, f32[3,96,768]{2,1,0:T(8,128)}, f32[24,768]{1,0:T(8,128)}) custom-call(bf16[96,192]{1,0:T(8,128)(2,1)} %WQ.1, bf16[96,192]{1,0:T(8,128)(2,1)} %WK.1, bf16[96,192]{1,0:T(8,128)(2,1)} %WV.1, bf16[192,96]{1,0:T(8,128)(2,1)} %WO.1, bf16[96,768]{1,0:T(8,128)(2,1)} %W1.1, ...), custom_call_target="tpu_custom_call" | custom-call | tf_op jit(solution)/shard_map/pallas_call | solution.py:820
  193.5 6.2 %shard_map.306 = (bf16[2048,768]{1,0:T(8,128)(2,1)}, bf16[2048,768]{1,0:T(8,128)(2,1)}, f32[96,192]{1,0:T(8,128)}, f32[96,192]{1,0:T(8,128)}, f32[96,192]{1,0:T(...) custom-call(bf16[2048,768]{1,0:T(8,128)(2,1)} %get-tuple-element.38., ...), custom_call_target="tpu_custom_call" | custom-call | tf_op jit(solution)/shard_map/pallas_call | solution.py:933
